TPU v7x, 32 devices: a whole 2x2x4 slice. The times are simulated.
32 devices in a mesh: groups: 2 (over y), scanx: 4 (over z), scany: 2 (over x), pos: 2 (over core).
Axes of the slice: x: 2, y: 2, z: 4, core: 2. Of those that a mesh axis runs over, the one named last changes fastest.
Arguments:
- specimen: float32 [2, 2048, 512], P(None, ('groups', 'scanx'), 'scany'), parts along dimension 1, may hold values from -5 to 5
- probe_wave: float32 [2, 512, 256], P(None, 'groups'), parts along dimension 1, may hold values from -6 to 6
- amplitudes: bfloat16 [64, 256, 256], P(('groups', 'scanx', 'scany', 'pos')), parts along dimension 0, may hold values from 0 to 2
- offsets: int32 [64, 2], P(('groups', 'scanx', 'scany', 'pos')), parts along dimension 0, may hold values from 0 to 255
Outputs:
- new_specimen: float32 [2, 2048, 512], P(None, ('groups', 'scanx'), 'scany'), parts along dimension 1
- new_probe: float32 [2, 512, 256], P(None, 'groups'), parts along dimension 1
There are 2 independent parts, one for each index of `groups`. A program takes and returns all parts, laid end to end along the dimension named above; each array names one. Nothing has to cross between parts.
Inputs may be any that keep to these rules, and one draw needn't show every extreme that they name: offsets are pixels from the top-left corner of the position's tile.
All inputs are finite; a program needn't handle non-finite values.
Results may differ from a plain program's by a relative error of at most 0.002.
The roundings to bfloat16 on the way count: a program that leaves them out, or rounds other values in their place, can miss the bound.
Values sent between devices are 32-bit elements; how exact they have to be, the bound alone decides.
A program may use at most 64 MiB of HBM per device.

v0:
```python
import functools
import math

import jax
import jax.numpy as jnp
import numpy as np
from jax import lax
from jax.experimental import pallas as pl
from jax.experimental.pallas import tpu as pltpu
from jax.sharding import PartitionSpec as P

MESH = pl.DeviceIdType.MESH
VMEM = pltpu.VMEM


def remote(src, dst, send, recv, where):
    return pltpu.make_async_remote_copy(
        src_ref=src, dst_ref=dst, send_sem=send, recv_sem=recv, device_id=where, device_id_type=MESH
    )


def greet(conditions_devices):
    barrier = pltpu.get_barrier_semaphore()
    for present, where in conditions_devices:
        if present is True:
            pl.semaphore_signal(barrier, inc=1, device_id=where, device_id_type=MESH)
        else:

            @pl.when(present)
            def _(where=where):
                pl.semaphore_signal(barrier, inc=1, device_id=where, device_id_type=MESH)

    fixed = sum(1 for present, _ in conditions_devices if present is True)
    peers = [present.astype(jnp.int32) for present, _ in conditions_devices if present is not True]
    pl.semaphore_wait(barrier, sum(peers, fixed))


class Side:
    def __init__(self, axis, count, step):
        me = lax.axis_index(axis)
        self.has = me > 0 if step < 0 else me < count - 1
        self.where = {axis: me + step}


class Role:
    def __init__(self, q, nx, ny):
        along_x = ("scanx", nx, Side("scanx", nx, -1), Side("scanx", nx, 1))
        along_y = ("scany", ny, Side("scany", ny, -1), Side("scany", ny, 1))
        one, two = (along_y, along_x) if q == 0 else (along_x, along_y)
        self.q, self.o, self.rows_first = q, 1 - q, q == 1
        self.axis1, self.n1, self.sides1 = one[0], one[1], one[2:]
        self.axis2, self.n2, self.sides2 = two[0], two[1], two[2:]
        self.me1, self.me2 = lax.axis_index(self.axis1), lax.axis_index(self.axis2)


def when(*conditions):
    return pl.when(functools.reduce(jnp.logical_and, conditions))


def dot(a, b):
    return jnp.dot(a, b, preferred_element_type=jnp.float32)


class Halo:
    def __init__(self, role, spec, pad, send, recv, partner):
        self.r, self.spec, self.pad, self.partner = role, spec, pad, partner
        self.send, self.recv = send, recv
        tile = spec.shape[1]
        half = (pad.shape[1] - tile) // 2
        self.own = pl.ds(half, tile)
        self.margins = (pl.ds(0, half), pl.ds(half + tile, half))
        self.edges = (pl.ds(0, half), pl.ds(tile - half, half))
        self.pad_edges = (pl.ds(half, half), pl.ds(tile, half))
        self.whole = pl.ds(0, tile)

    def at(self, one, two):
        return (self.r.q, one, two) if self.r.rows_first else (self.r.q, two, one)

    def copy(self, src, dst, i, where):
        return remote(src, dst, self.send.at[i], self.recv.at[i], where)

    def strip1(self, m):
        return self.copy(
            self.spec.at[self.at(self.edges[1 - m], self.whole)],
            self.pad.at[self.at(self.margins[m], self.own)],
            m,
            self.r.sides1[1 - m].where,
        )

    def strip2(self, m):
        return self.copy(
            self.spec.at[self.at(self.whole, self.edges[1 - m])],
            self.pad.at[self.at(self.own, self.margins[m])],
            2 + m,
            self.r.sides2[1 - m].where,
        )

    def corner(self, m1, m2):
        return self.copy(
            self.pad.at[self.at(self.margins[m1], self.pad_edges[1 - m2])],
            self.pad.at[self.at(self.margins[m1], self.margins[m2])],
            4 + 2 * m1 + m2,
            self.r.sides2[1 - m2].where,
        )

    def share(self, i, one, two):
        ref = self.pad.at[self.at(one, two)]
        return self.copy(ref, ref, 8 + i, self.partner)

    def share1(self, m):
        return self.share(m, self.margins[m], self.own)

    def share2(self, m):
        return self.share(2 + m, self.own, self.margins[m])

    def share_corner(self, m1, m2):
        return self.share(4 + 2 * m1 + m2, self.margins[m1], self.margins[m2])

    def begin(self):
        for m in range(2):
            when(self.r.sides1[1 - m].has)(self.strip1(m).start)
        for m in range(2):
            when(self.r.sides2[1 - m].has)(self.strip2(m).start)

    def relay(self):
        r = self.r
        for m1 in range(2):

            @when(r.sides1[m1].has)
            def _():
                self.strip1(m1).wait_recv()
                for m2 in range(2):
                    when(r.sides2[1 - m2].has)(self.corner(m1, m2).start)
                self.share1(m1).start()

        for m in range(2):

            @when(r.sides2[m].has)
            def _():
                self.strip2(m).wait_recv()
                self.share2(m).start()

        for m1 in range(2):
            for m2 in range(2):

                @when(r.sides1[m1].has, r.sides2[m2].has)
                def _():
                    self.corner(m1, m2).wait_recv()
                    self.share_corner(m1, m2).start()

    def arrive(self):
        r = self.r
        for m in range(2):
            when(r.sides1[m].has)(self.share1(m).wait_recv)
            when(r.sides2[m].has)(self.share2(m).wait_recv)
        for m1 in range(2):
            for m2 in range(2):
                when(r.sides1[m1].has, r.sides2[m2].has)(self.share_corner(m1, m2).wait_recv)

    def finish(self):
        r = self.r
        for m in range(2):
            when(r.sides1[1 - m].has)(self.strip1(m).wait_send)
            when(r.sides2[1 - m].has)(self.strip2(m).wait_send)
            when(r.sides1[m].has)(self.share1(m).wait_send)
            when(r.sides2[m].has)(self.share2(m).wait_send)
        for m1 in range(2):
            for m2 in range(2):
                when(r.sides1[m1].has, r.sides2[1 - m2].has)(self.corner(m1, m2).wait_send)
                when(r.sides1[m1].has, r.sides2[m2].has)(self.share_corner(m1, m2).wait_send)


class Fold:
    def __init__(self, role, mine, theirs, pair, acc, rims, core, send, recv, partner):
        self.r, self.mine, self.theirs, self.pair, self.acc = role, mine, theirs, pair, acc
        self.xr1, self.xr2, self.zr1, self.zr2 = rims
        self.core, self.send, self.recv, self.partner = core, send, recv, partner
        w = acc.shape[-1]
        self.w, self.q4 = w, w // 4

    def pieces(self, rows):
        q4, w = self.q4, self.w
        if rows:
            return [(pl.ds(0, 1),), (pl.ds(3, 1),), (pl.ds(1, 2),)]
        lead = (slice(None),) * 3
        return [lead + (pl.ds(0, q4),), lead + (pl.ds(3 * q4, q4),), lead + (pl.ds(q4, 2 * q4),)]

    def pair_copy(self, i, rows):
        at = self.pieces(rows)[i]
        return remote(self.theirs.at[at], self.pair.at[at], self.send.at[i], self.recv.at[i], self.partner)

    def begin(self):
        for i in range(3):
            self.pair_copy(i, not self.r.rows_first).start()

    def add(self, i):
        self.pair_copy(i, self.r.rows_first).wait_recv()
        at = self.pieces(self.r.rows_first)[i]
        self.acc[at] = self.mine[at] + self.pair[at]

    def rim_copy(self, stage, m):
        r, q4, w = self.r, self.q4, self.w
        rows = r.rows_first == (stage == 0)
        k = 1 - m
        if rows:
            cols = pl.ds(0, w) if stage == 0 else pl.ds(q4, 2 * q4)
            src = self.acc.at[3 * k, :, :, cols]
            rim = self.zr1 if stage == 0 else self.zr2
        else:
            groups = pl.ds(0, 4) if stage == 0 else pl.ds(1, 2)
            src = self.acc.at[groups, :, :, pl.ds(3 * k * q4, q4)]
            rim = self.xr1 if stage == 0 else self.xr2
        sides = r.sides1 if stage == 0 else r.sides2
        i = 3 + 2 * stage + m
        return remote(src, rim.at[m], self.send.at[i], self.recv.at[i], sides[k].where)

    def send_rims(self, stage):
        sides = self.r.sides1 if stage == 0 else self.r.sides2
        for m in range(2):
            when(sides[1 - m].has)(self.rim_copy(stage, m).start)

    def fold(self, stage):
        r, q4, w, acc = self.r, self.q4, self.w, self.acc
        rows = r.rows_first == (stage == 0)
        sides = r.sides1 if stage == 0 else r.sides2
        for m in range(2):

            @when(sides[m].has)
            def _():
                self.rim_copy(stage, m).wait_recv()
                if rows:
                    cols = pl.ds(0, w) if stage == 0 else pl.ds(q4, 2 * q4)
                    rim = self.zr1 if stage == 0 else self.zr2
                    acc[1 + m, :, :, cols] = acc[1 + m, :, :, cols] + rim[m]
                else:
                    groups = pl.ds(0, 4) if stage == 0 else pl.ds(1, 2)
                    cols = pl.ds((1 + m) * q4, q4)
                    rim = self.xr1 if stage == 0 else self.xr2
                    acc[groups, :, :, cols] = acc[groups, :, :, cols] + rim[m]

    def share_copy(self, q):
        return remote(self.core.at[q], self.core.at[q], self.send.at[7], self.recv.at[7], self.partner)

    def share(self):
        q4 = self.q4
        self.core[self.r.q] = self.acc[1:3, :, :, q4 : 3 * q4]
        self.share_copy(self.r.q).start()

    def arrive(self):
        self.share_copy(self.r.o).wait_recv()

    def finish(self):
        r = self.r
        for i in range(3):
            self.pair_copy(i, not r.rows_first).wait_send()
        for m in range(2):
            when(r.sides1[1 - m].has)(self.rim_copy(0, m).wait_send)
            when(r.sides2[1 - m].has)(self.rim_copy(1, m).wait_send)
        self.share_copy(r.q).wait_send()


class ProbeSum:
    def __init__(self, role, mine, theirs, ppair, pacc, p1, pr1, pr2, total, send, recv, partner):
        self.r, self.mine, self.theirs = role, mine, theirs
        self.ppair, self.pacc, self.p1 = ppair, pacc, p1
        self.pr1, self.pr2, self.total = pr1, pr2, total
        self.send, self.recv, self.partner = send, recv, partner

    def copy(self, src, dst, stage, d, where):
        return remote(src, dst, self.send.at[stage, d], self.recv.at[stage, d], where)

    def pair_copy(self):
        return self.copy(self.theirs, self.ppair, 0, 0, self.partner)

    def begin(self):
        self.pair_copy().start()

    def scatter1(self):
        r = self.r
        out = []
        for d in range(1, r.n1):
            j = lax.rem(r.me1 + d, r.n1)
            src = self.pacc.at[pl.ds(j * r.n2, r.n2)]
            out.append(self.copy(src, self.pr1.at[pl.ds(d * r.n2, r.n2)], 1, d, {r.axis1: j}))
        return out

    def scatter2(self):
        r = self.r
        out = []
        for d in range(1, r.n2):
            j = lax.rem(r.me2 + d, r.n2)
            out.append(self.copy(self.p1.at[pl.ds(j, 1)], self.pr2.at[pl.ds(d, 1)], 2, d, {r.axis2: j}))
        return out

    def gather2(self, back):
        r = self.r
        out = []
        for d in range(1, r.n2):
            j = lax.rem(r.me2 + d, r.n2)
            origin = lax.rem(r.me2 - d + r.n2, r.n2) if back else r.me2
            ref = self.total.at[r.q, pl.ds(r.me1 * r.n2 + origin, 1)]
            out.append(self.copy(ref, ref, 3, d, {r.axis2: j}))
        return out

    def gather1(self, back):
        r = self.r
        out = []
        for d in range(1, r.n1):
            j = lax.rem(r.me1 + d, r.n1)
            origin = lax.rem(r.me1 - d + r.n1, r.n1) if back else r.me1
            ref = self.total.at[r.q, pl.ds(origin * r.n2, r.n2)]
            out.append(self.copy(ref, ref, 4, d, {r.axis1: j}))
        return out

    def share_copy(self, d, sender):
        r = self.r
        origin = lax.rem(r.me1 - d + r.n1, r.n1)
        ref = self.total.at[r.q, pl.ds(origin * r.n2, r.n2)]
        return self.copy(ref, ref, 5, d, self.partner)

    def step1(self):
        self.pair_copy().wait_recv()
        self.pacc[...] = self.mine[...] + self.ppair[...]
        for c in self.scatter1():
            c.start()

    def step2(self):
        r = self.r
        mine = self.pacc[pl.ds(r.me1 * r.n2, r.n2)]
        for d, c in enumerate(self.scatter1(), 1):
            c.wait_recv()
            mine = mine + self.pr1[d * r.n2 : (d + 1) * r.n2]
        self.p1[0 : r.n2] = mine
        for c in self.scatter2():
            c.start()

    def step3(self):
        r = self.r
        one = self.p1[pl.ds(r.me2, 1)]
        for d, c in enumerate(self.scatter2(), 1):
            c.wait_recv()
            one = one + self.pr2[d : d + 1]
        self.total[r.q, pl.ds(r.me1 * r.n2 + r.me2, 1)] = one
        for c in self.gather2(0):
            c.start()

    def step4(self):
        for c in self.gather2(1):
            c.wait_recv()
        for c in self.gather1(0):
            c.start()
        self.share_copy(0, True).start()

    def step5(self):
        for d, c in enumerate(self.gather1(1), 1):
            c.wait_recv()
            self.share_copy(d, True).start()

    def arrive(self):
        for d in range(self.r.n1):
            self.share_copy(d, False).wait_recv()

    def finish(self):
        self.pair_copy().wait_send()
        for c in self.scatter1() + self.scatter2() + self.gather2(0) + self.gather1(0):
            c.wait_send()
        for d in range(self.r.n1):
            self.share_copy(d, True).wait_send()


def line_greet(nx, ny, partner):
    mx, my = lax.axis_index("scanx"), lax.axis_index("scany")
    greet(
        [(True, partner)]
        + [(True, {"scanx": lax.rem(mx + d, nx)}) for d in range(1, nx)]
        + [(True, {"scany": lax.rem(my + d, ny)}) for d in range(1, ny)]
    )


def each(step):
    p = lax.axis_index("pos")
    for q in range(2):
        pl.when(p == q)(functools.partial(step, q))


def halo_kernel(nx, ny, spec, *refs):
    loaded, pad, kept = refs[:5], refs[5], refs[6:11]
    send, recv, local = refs[11:]
    tile = spec.shape[1]
    half = (pad.shape[1] - tile) // 2
    own = pl.ds(half, tile)
    partner = {"pos": 1 - lax.axis_index("pos")}
    loads = [pltpu.make_async_copy(spec, pad.at[:, own, own], local.at[0])]
    for i, (src, dst) in enumerate(zip(loaded, kept), 1):
        loads.append(pltpu.make_async_copy(src, dst, local.at[i]))
    for c in loads:
        c.start()
    roles = [Role(q, nx, ny) for q in range(2)]
    sides = roles[1].sides1 + roles[0].sides1
    greet([(True, partner)] + [(side.has, side.where) for side in sides])
    halos = [Halo(r, spec, pad, send, recv, partner) for r in roles]
    each(lambda q: halos[q].begin())
    for i, at in enumerate(
        (
            (slice(None), pl.ds(0, half)),
            (slice(None), pl.ds(half + tile, half)),
            (slice(None), slice(None), pl.ds(0, half)),
            (slice(None), slice(None), pl.ds(half + tile, half)),
        )
    ):

        @pl.when(jnp.logical_not(sides[i].has))
        def _(at=at):
            pad[at] = jnp.zeros(pad.at[at].shape, pad.dtype)

    def rest(q):
        halos[q].relay()
        halos[1 - q].arrive()
        halos[q].finish()

    each(rest)
    for c in loads:
        c.wait()


def step_kernel(offsets, pad, probe, amplitudes, table_a, table_b, grad, prob):
    m = probe.shape[1]
    tall, span = m + 8, m + 128
    pr, pi = probe[0], probe[1]
    grad[...] = jnp.zeros(grad.shape, grad.dtype)
    blank_rows = jnp.zeros((tall - m, m), jnp.float32)
    blank_cols = jnp.zeros((tall, span - m), jnp.float32)
    bf = jnp.bfloat16
    positions = amplitudes.shape[0]

    def place_at(j):
        row, col = offsets[j, 0], offsets[j, 1]
        row_in, col_in = lax.rem(row, 8), lax.rem(col, 128)
        rows = pl.ds(pl.multiple_of(row - row_in, 8), tall)
        cols = pl.ds(pl.multiple_of(col - col_in, 128), span)
        return row_in, col_in, rows, cols

    def place(j, k, term):
        row_in, col_in, rows, cols = place_at(j)
        moved = pltpu.roll(jnp.concatenate([term, blank_rows], 0), row_in, 0)
        moved = pltpu.roll(jnp.concatenate([moved, blank_cols], 1), col_in, 1)
        grad[k, rows, cols] = grad[k, rows, cols] + moved

    power = pr * pr + pi * pi
    for j in range(positions):
        place(j, 2, power)
    sum_r = sum_i = None
    for j in range(positions):
        row_in, col_in, rows, cols = place_at(j)

        def window(k):
            block = pad[k, rows, cols]
            block = pltpu.roll(block, lax.rem(span - col_in, span), 1)[:, :m]
            return pltpu.roll(block, lax.rem(tall - row_in, tall), 0)[:m]

        ar, ai = window(0), window(1)
        er = pr * ar - pi * ai
        ei = pr * ai + pi * ar
        left = dot(table_a[...], jnp.concatenate([er.astype(bf), ei.astype(bf)], 0)).astype(bf)
        far = dot(jnp.concatenate([left[:m], left[m:]], 1), table_b[...])
        fr, fi = far[:, :m], far[:, m:]
        ratio = amplitudes[j].astype(jnp.float32) / jnp.maximum(jnp.sqrt(fr * fr + fi * fi), 0.2)
        projected = jnp.concatenate([(fr * ratio).astype(bf), (fi * ratio).astype(bf)], 0)
        back_half = dot(table_b[...], projected).astype(bf)
        back = dot(jnp.concatenate([back_half[:m], back_half[m:]], 1), table_a[...])
        dr = back[:, :m] - er
        di = back[:, m:] - ei
        tr = ar * dr + ai * di
        ti = ar * di - ai * dr
        sum_r = tr if sum_r is None else sum_r + tr
        sum_i = ti if sum_i is None else sum_i + ti
        place(j, 0, pr * dr + pi * di)
        place(j, 1, pr * di - pi * dr)
    n, s, lanes = prob.shape[1:]
    for k, value in enumerate((sum_r, sum_i)):
        for c in range(n):
            r0, l0 = c * s % m, c * s // m * lanes
            prob[k, c] = value[r0 : r0 + s, l0 : l0 + lanes]


def reduce_kernel(nx, ny, *refs):
    grad, prob, core, icore, total = refs[:5]
    (pair, acc, xr1, xr2, zr1, zr2, ipair, iacc, ixr1, ixr2, izr1, izr2) = refs[5:17]
    (ppair, pacc, p1, pr1, pr2) = refs[17:22]
    (gsend, grecv, isend, irecv, psend, precv) = refs[22:]
    p = lax.axis_index("pos")
    partner = {"pos": 1 - p}
    line_greet(nx, ny, partner)
    roles = [Role(q, nx, ny) for q in range(2)]
    folds = [
        Fold(r, grad.at[r.q], grad.at[r.o], pair, acc, (xr1, xr2, zr1, zr2), core, gsend, grecv, partner)
        for r in roles
    ]
    lights = [
        Fold(
            r,
            grad.at[2, :, pl.ds(r.q, 1)],
            grad.at[2, :, pl.ds(r.o, 1)],
            ipair,
            iacc,
            (ixr1, ixr2, izr1, izr2),
            icore,
            isend,
            irecv,
            partner,
        )
        for r in roles
    ]
    probes = [
        ProbeSum(r, prob.at[r.q], prob.at[r.o], ppair, pacc, p1, pr1, pr2, total, psend, precv, partner)
        for r in roles
    ]

    def objects(q):
        probe_sum, fold, light = probes[q], folds[q], lights[q]
        probe_sum.begin()
        fold.begin()
        light.begin()
        probe_sum.step1()
        fold.add(0)
        fold.add(1)
        fold.send_rims(0)
        light.add(0)
        light.add(1)
        light.send_rims(0)
        fold.add(2)
        light.add(2)
        probe_sum.step2()
        fold.fold(0)
        fold.send_rims(1)
        light.fold(0)
        light.send_rims(1)
        probe_sum.step3()
        fold.fold(1)
        fold.share()
        light.fold(1)
        light.share()
        probe_sum.step4()
        light.arrive()
        fold.arrive()

    each(objects)
    def closing(q):
        probes[q].step5()
        probes[1 - q].arrive()
        lights[q].finish()
        folds[q].finish()
        probes[q].finish()

    each(closing)

def apply_kernel(step_size, core, light, total, pad, probe, new_spec, new_probe):
    tile = new_spec.shape[1]
    half = (pad.shape[1] - tile) // 2
    m = probe.shape[1]
    h = core.shape[3]
    for k in range(2):
        for g in range(2):
            for b in range(2):
                r0 = (2 * g + b) * h
                old = pad[k, half + r0 : half + r0 + h, half : half + tile]
                new_spec[k, r0 : r0 + h] = old + core[k, g, b] / (light[b, g, 0] + 1.0)
    n, s, lanes = total.shape[1:]
    for k in range(2):
        for c in range(n):
            rows = slice(c * s % m, c * s % m + s)
            cols = slice(c * s // m * lanes, c * s // m * lanes + lanes)
            new_probe[k, rows, cols] = probe[k, rows, cols] + total[k, c] * step_size


def tables(length):
    index = np.arange(length)
    angle = ((index[:, None] * index[None, :]) % length).astype(np.float32) * np.float32(2.0 * math.pi / length)
    scale = np.float32(1.0 / math.sqrt(length))
    c = np.cos(angle) * scale
    s = np.sin(angle) * scale
    a = np.block([[c, s], [-s, c]]).astype(jnp.bfloat16)
    b = np.block([[c, -s], [s, c]]).astype(jnp.bfloat16)
    return a, b


def shards(nx, ny, consts, specimen, probe_wave, amplitudes, offsets):
    m = probe_wave.shape[1]
    tile = specimen.shape[1]
    wide = tile + m
    f32 = jnp.float32
    vm = pl.BlockSpec(memory_space=VMEM)
    sm = pl.BlockSpec(memory_space=pltpu.SMEM)
    anywhere = pl.BlockSpec(memory_space=pl.ANY)
    dma = pltpu.SemaphoreType.DMA
    lanes = 128
    n = nx * ny
    s = m * m // lanes // n
    h = wide // 8
    most = max(nx, ny)
    positions = offsets.shape[0]
    shaped = VMEM
    held = (offsets, probe_wave, amplitudes, consts[0], consts[1])
    hbm = pl.BlockSpec(memory_space=pltpu.HBM)
    pad, *held = pl.pallas_call(
        functools.partial(halo_kernel, nx, ny),
        out_shape=[shaped((2, wide, wide), f32)] + [shaped(x.shape, x.dtype) for x in held],
        in_specs=[hbm] * 6,
        out_specs=[vm] * 6,
        scratch_shapes=[dma((16,)), dma((16,)), dma((6,))],
        compiler_params=pltpu.CompilerParams(vmem_limit_bytes=16 * 2**20, collective_id=0, has_side_effects=True),
        name="halo",
    )(*[pltpu.with_memory_space_constraint(x, pltpu.HBM) for x in (specimen, *held)])
    grad, prob = pl.pallas_call(
        step_kernel,
        out_shape=[
            jax.ShapeDtypeStruct((3, wide, wide), f32),
            jax.ShapeDtypeStruct((2, n, s, lanes), f32),
        ],
        in_specs=[sm] + [vm] * 5,
        out_specs=[vm, vm],
        compiler_params=pltpu.CompilerParams(vmem_limit_bytes=32 * 2**20),
        name="step",
    )(held[0], pad, *held[1:])

    def field(size):
        return [
            VMEM((4, size, h, wide), f32),
            VMEM((4, size, h, wide), f32),
            VMEM((2, 4, size, h, wide // 4), f32),
            VMEM((2, 2, size, h, wide // 4), f32),
            VMEM((2, size, h, wide), f32),
            VMEM((2, size, h, wide // 2), f32),
        ]

    step_size = 1.0 / math.sqrt(positions * n * 2)
    core, light, total = pl.pallas_call(
        functools.partial(reduce_kernel, nx, ny),
        out_shape=[
            shaped((2, 2, 2, h, wide // 2), f32),
            shaped((2, 2, 1, h, wide // 2), f32),
            shaped((2, n, s, lanes), f32),
        ],
        in_specs=[vm] * 2,
        out_specs=[vm, vm, vm],
        scratch_shapes=[
            *field(2),
            *field(1),
            VMEM((n, s, lanes), f32),
            VMEM((n, s, lanes), f32),
            VMEM((most, s, lanes), f32),
            VMEM((n, s, lanes), f32),
            VMEM((most, s, lanes), f32),
            dma((8,)),
            dma((8,)),
            dma((8,)),
            dma((8,)),
            dma((6, most)),
            dma((6, most)),
        ],
        compiler_params=pltpu.CompilerParams(vmem_limit_bytes=32 * 2**20, collective_id=1, has_side_effects=True),
        name="reduce",
    )(grad.reshape(3, 4, 2, h, wide), prob)
    return pl.pallas_call(
        functools.partial(apply_kernel, step_size),
        out_shape=[
            jax.ShapeDtypeStruct(specimen.shape, f32),
            jax.ShapeDtypeStruct(probe_wave.shape, f32),
        ],
        in_specs=[vm] * 5,
        out_specs=[vm, vm],
        compiler_params=pltpu.CompilerParams(vmem_limit_bytes=16 * 2**20),
        name="apply",
    )(core, light, total, pad, held[1])


def solution(mesh):
    nx, ny = mesh.shape["scanx"], mesh.shape["scany"]

    def run(specimen, probe_wave, amplitudes, offsets):
        consts = tables(probe_wave.shape[2])
        return jax.shard_map(
            lambda *args: shards(nx, ny, [jnp.asarray(t) for t in consts], *args),
            mesh=mesh,
            in_specs=(
                P(None, ("groups", "scanx"), "scany"),
                P(None, "groups", None),
                P(("groups", "scanx", "scany", "pos"), None, None),
                P(("groups", "scanx", "scany", "pos"), None),
            ),
            out_specs=(P(None, ("groups", "scanx"), "scany"), P(None, "groups", None)),
            check_vma=False,
        )(specimen, probe_wave, amplitudes, offsets)

    return run
```

profile of v0, /device:TPU:0, one launch (start us, length us, event | category | flops | bytes accessed | tf_op | source)
XLA Modules:
  0.0 42.5 jit_solution(14622753364608919350)
XLA Ops:
  0.6 13.1 %halo.1 = (f32[2,512,512]{2,1,0:T(8,128)S(1)}, s32[2,2]{1,0:T(2,128)S(1)}, f32[2,256,256]{2,1,0:T(8,128)S(1)}, bf16[2,256,256]{2,1,0:T(8,128)(2,1)S(1)}, bf16[51...) custom-call(f32[2,256,256]{2,1,0:T(8,128)} %spec.1, s32[2,2]{1,0:T(2,128)} %refs_0_.1, f32[2,256,256]{2,1,0:T(8,128)} %refs_1_.1, ...), custom_call_target="tpu_custom_call" | custom-call | tf_op jit(solution)/shard_map/halo/pallas_call | solution.py:605
  13.8 4.8 %step.1 = (f32[3,512,512]{2,1,0:T(8,128)S(1)}, f32[2,8,64,128]{3,2,1,0:T(8,128)S(1)}) custom-call(s32[2,2]{1,0:T(2,128)S(1)} %get-tuple-element.13.offsets, f32[2,512,512]{2,1,0:T(8,128)S(1)} %get-tuple-element.14.pad, f32[2,256,256]{2,1,0:T(8,128)S(1)} %get-tuple-element.15.probe, bf16[2,256,256]{2,1,0:T(8,128)(2,1)S(1)} %get-tuple-element.16.amplitudes, ...), custom_call_target="tpu_custom_call" | custom-call | tf_op jit(solution)/shard_map/step/pallas_call | solution.py:614
  18.6 22.7 %reduce.1 = (f32[2,2,2,64,256]{4,3,2,1,0:T(8,128)S(1)}, f32[2,2,1,64,256]{4,3,2,1,0:T(8,128)S(1)}, f32[2,8,64,128]{3,2,1,0:T(8,128)S(1)}) custom-call(f32[3,4,2,64,512]{4,3,2,1,0:T(8,128)S(1)} %bitcast.1, f32[2,8,64,128]{3,2,1,0:T(8,128)S(1)} %get-tuple-element.20.refs_1_), custom_call_target="tpu_custom_call" | custom-call | tf_op jit(solution)/shard_map/reduce/pallas_call | solution.py:637
  41.3 1.1 %apply.1 = (f32[2,256,256]{2,1,0:T(8,128)}, f32[2,256,256]{2,1,0:T(8,128)}) custom-call(f32[2,2,2,64,256]{4,3,2,1,0:T(8,128)S(1)} %get-tuple-element.21.core, f32[2,2,1,64,256]{4,3,2,1,0:T(8,128)S(1)} %get-tuple-element.22.light, f32[2,8,64,128]{3,2,1,0:T(8,128)S(1)} %get-tuple-element.23.total, f32[2,512,512]{2,1,0:T(8,128)S(1)} %get-tuple-element.14.pad, ...), custom_call_target="tpu_custom_call" | custom-call | tf_op jit(solution)/shard_map/apply/pallas_call | solution.py:664
where the time goes:
time: 42.6 us; the launch traced here: 42.5 us
  Pallas kernels  41.8 us (98%)
  between operations  0.65 us (2%)
    pallas_call x1, Pallas kernels, shards(): pl.pallas_call(functools.partial(reduce_kernel, nx, ny), out_shape=[shape...  22.7 us
    pallas_call x1, Pallas kernels, shards(): pl.pallas_call(functools.partial(halo_kernel, nx, ny), out_shape=[shaped(...  13.1 us
    pallas_call x1, Pallas kernels, shards(): pl.pallas_call(step_kernel, out_shape=[jax.ShapeDtypeStruct((3, wide, wid...  4.81 us
    pallas_call x1, Pallas kernels, shards(): pl.pallas_call(functools.partial(apply_kernel, step_size), out_shape=[jax...  1.14 us

commit v1 on v0

--- a/solution.py
+++ b/solution.py
@@ -65,16 +65,17 @@
     def __init__(self, role, spec, pad, send, recv, partner):
         self.r, self.spec, self.pad, self.partner = role, spec, pad, partner
         self.send, self.recv = send, recv
-        tile = spec.shape[1]
-        half = (pad.shape[1] - tile) // 2
-        self.own = pl.ds(half, tile)
-        self.margins = (pl.ds(0, half), pl.ds(half + tile, half))
-        self.edges = (pl.ds(0, half), pl.ds(tile - half, half))
-        self.pad_edges = (pl.ds(half, half), pl.ds(tile, half))
-        self.whole = pl.ds(0, tile)
+        tile = spec.shape[3]
+        half = (pad.shape[3] - tile) // 2
+        self.own = (half, tile)
+        self.margins = ((0, half), (half + tile, half))
+        self.edges = ((0, half), (tile - half, half))
+        self.pad_edges = ((half, half), (tile, half))
+        self.whole = (0, tile)
 
     def at(self, one, two):
-        return (self.r.q, one, two) if self.r.rows_first else (self.r.q, two, one)
+        rows, cols = (one, two) if self.r.rows_first else (two, one)
+        return (self.r.q, pl.ds(rows[0] // 8, rows[1] // 8), slice(None), pl.ds(*cols))
 
     def copy(self, src, dst, i, where):
         return remote(src, dst, self.send.at[i], self.recv.at[i], where)
@@ -256,7 +257,8 @@
         for m in range(2):
             when(r.sides1[1 - m].has)(self.rim_copy(0, m).wait_send)
             when(r.sides2[1 - m].has)(self.rim_copy(1, m).wait_send)
-        self.share_copy(r.q).wait_send()
+        if self.core is not None:
+            self.share_copy(r.q).wait_send()
 
 
 class ProbeSum:
@@ -383,117 +385,97 @@
         pl.when(p == q)(functools.partial(step, q))
 
 
-def halo_kernel(nx, ny, spec, *refs):
-    loaded, pad, kept = refs[:5], refs[5], refs[6:11]
-    send, recv, local = refs[11:]
-    tile = spec.shape[1]
-    half = (pad.shape[1] - tile) // 2
-    own = pl.ds(half, tile)
-    partner = {"pos": 1 - lax.axis_index("pos")}
-    loads = [pltpu.make_async_copy(spec, pad.at[:, own, own], local.at[0])]
-    for i, (src, dst) in enumerate(zip(loaded, kept), 1):
+class Placer:
+    def __init__(self, offsets, bufs, m, positions):
+        self.bufs, self.m = bufs, m
+        self.tall, self.span = m + 8, m + 128
+        self.top = (bufs.shape[2] - self.tall // 8) // 2
+        self.spots = []
+        for j in range(positions):
+            row, col = offsets[j, 0], offsets[j, 1]
+            self.spots.append((lax.rem(row, 8), lax.rem(col, 128), lax.div(row, 8), lax.div(col, 128)))
+
+    def clear(self):
+        n, k, rows = self.bufs.shape[:3]
+        bottom = self.top + self.tall // 8
+        for j in range(n):
+            for c in range(k):
+                self.bufs[j, c, 0 : self.top] = jnp.zeros((self.top, *self.bufs.shape[3:]), jnp.float32)
+                self.bufs[j, c, bottom:rows] = jnp.zeros((rows - bottom, *self.bufs.shape[3:]), jnp.float32)
+
+    def put(self, j, k, term):
+        row_in, col_in, _, step = self.spots[j]
+        m, wide = self.m, self.bufs.shape[4]
+        blank_rows = jnp.zeros((self.tall - m, m), jnp.float32)
+        blank_cols = jnp.zeros((self.tall, self.span - m), jnp.float32)
+        moved = pltpu.roll(jnp.concatenate([term, blank_rows], 0), row_in, 0)
+        moved = pltpu.roll(jnp.concatenate([moved, blank_cols], 1), col_in, 1)
+        out = None
+        for d in range((wide - self.span) // 128 + 1):
+            parts = [jnp.zeros((self.tall, w), jnp.float32) for w in (128 * d, wide - self.span - 128 * d)]
+            here = jnp.concatenate([x for x in (parts[0], moved, parts[1]) if x.shape[1]], 1)
+            out = here if out is None else jnp.where(step == d, here, out)
+        self.bufs[j, k, self.top : self.top + self.tall // 8] = out.reshape(self.tall // 8, 8, wide)
+
+    def rows(self, k, r0, count):
+        out = None
+        for j, (_, _, row, _) in enumerate(self.spots):
+            part = self.bufs[j, k, pl.ds(self.top - row + r0 // 8, count // 8)]
+            out = part if out is None else out + part
+        return out.reshape(count, self.bufs.shape[4])
+
+    def window(self, j, pad, k):
+        row_in, col_in, row, step = self.spots[j]
+        wide = pad.shape[3]
+        block = pad[k, pl.ds(row, self.tall // 8)].reshape(self.tall, wide)
+        out = block[:, : self.span]
+        for d in range(1, (wide - self.span) // 128 + 1):
+            out = jnp.where(step == d, block[:, 128 * d : 128 * d + self.span], out)
+        out = pltpu.roll(out, lax.rem(self.span - col_in, self.span), 1)[:, : self.m]
+        return pltpu.roll(out, lax.rem(self.tall - row_in, self.tall), 0)[: self.m]
+
+
+def project(window, pr, pi, amplitude, table_a, table_b):
+    m = pr.shape[0]
+    bf = jnp.bfloat16
+    ar, ai = window
+    er = pr * ar - pi * ai
+    ei = pr * ai + pi * ar
+    left = dot(table_a[...], jnp.concatenate([er.astype(bf), ei.astype(bf)], 0)).astype(bf)
+    far = dot(jnp.concatenate([left[:m], left[m:]], 1), table_b[...])
+    fr, fi = far[:, :m], far[:, m:]
+    ratio = amplitude.astype(jnp.float32) / jnp.maximum(jnp.sqrt(fr * fr + fi * fi), 0.2)
+    projected = jnp.concatenate([(fr * ratio).astype(bf), (fi * ratio).astype(bf)], 0)
+    back_half = dot(table_b[...], projected).astype(bf)
+    back = dot(jnp.concatenate([back_half[:m], back_half[m:]], 1), table_a[...])
+    return back[:, :m] - er, back[:, m:] - ei
+
+
+def whole_kernel(nx, ny, step_size, *refs):
+    offsets, spec, *given = refs[:6]
+    new_spec, new_probe = refs[6:8]
+    pad, probe, amplitudes, table_a, table_b, bufs, grad, prob, total, light_all = refs[8:18]
+    (pair, acc, xr1, xr2, zr1, zr2, ipair, iacc, ixr1, ixr2, izr1, izr2) = refs[18:30]
+    (ppair, pacc, p1, pr1, pr2) = refs[30:35]
+    (hsend, hrecv, local, gsend, grecv, isend, irecv, psend, precv) = refs[35:]
+    tile, m = spec.shape[3], probe.shape[1]
+    wide = pad.shape[3]
+    half = (wide - tile) // 2
+    h = grad.shape[3]
+    positions = amplitudes.shape[0]
+    p = lax.axis_index("pos")
+    partner = {"pos": 1 - p}
+    loads = [pltpu.make_async_copy(spec, pad.at[:, pl.ds(half // 8, tile // 8), :, pl.ds(half, tile)], local.at[0])]
+    for i, (src, dst) in enumerate(zip(given, (probe, amplitudes, table_a, table_b)), 1):
         loads.append(pltpu.make_async_copy(src, dst, local.at[i]))
     for c in loads:
         c.start()
+    line_greet(nx, ny, partner)
     roles = [Role(q, nx, ny) for q in range(2)]
     sides = roles[1].sides1 + roles[0].sides1
-    greet([(True, partner)] + [(side.has, side.where) for side in sides])
-    halos = [Halo(r, spec, pad, send, recv, partner) for r in roles]
-    each(lambda q: halos[q].begin())
-    for i, at in enumerate(
-        (
-            (slice(None), pl.ds(0, half)),
-            (slice(None), pl.ds(half + tile, half)),
-            (slice(None), slice(None), pl.ds(0, half)),
-            (slice(None), slice(None), pl.ds(half + tile, half)),
-        )
-    ):
-
-        @pl.when(jnp.logical_not(sides[i].has))
-        def _(at=at):
-            pad[at] = jnp.zeros(pad.at[at].shape, pad.dtype)
-
-    def rest(q):
-        halos[q].relay()
-        halos[1 - q].arrive()
-        halos[q].finish()
-
-    each(rest)
-    for c in loads:
-        c.wait()
-
-
-def step_kernel(offsets, pad, probe, amplitudes, table_a, table_b, grad, prob):
-    m = probe.shape[1]
-    tall, span = m + 8, m + 128
-    pr, pi = probe[0], probe[1]
-    grad[...] = jnp.zeros(grad.shape, grad.dtype)
-    blank_rows = jnp.zeros((tall - m, m), jnp.float32)
-    blank_cols = jnp.zeros((tall, span - m), jnp.float32)
-    bf = jnp.bfloat16
-    positions = amplitudes.shape[0]
-
-    def place_at(j):
-        row, col = offsets[j, 0], offsets[j, 1]
-        row_in, col_in = lax.rem(row, 8), lax.rem(col, 128)
-        rows = pl.ds(pl.multiple_of(row - row_in, 8), tall)
-        cols = pl.ds(pl.multiple_of(col - col_in, 128), span)
-        return row_in, col_in, rows, cols
-
-    def place(j, k, term):
-        row_in, col_in, rows, cols = place_at(j)
-        moved = pltpu.roll(jnp.concatenate([term, blank_rows], 0), row_in, 0)
-        moved = pltpu.roll(jnp.concatenate([moved, blank_cols], 1), col_in, 1)
-        grad[k, rows, cols] = grad[k, rows, cols] + moved
-
-    power = pr * pr + pi * pi
-    for j in range(positions):
-        place(j, 2, power)
-    sum_r = sum_i = None
-    for j in range(positions):
-        row_in, col_in, rows, cols = place_at(j)
-
-        def window(k):
-            block = pad[k, rows, cols]
-            block = pltpu.roll(block, lax.rem(span - col_in, span), 1)[:, :m]
-            return pltpu.roll(block, lax.rem(tall - row_in, tall), 0)[:m]
-
-        ar, ai = window(0), window(1)
-        er = pr * ar - pi * ai
-        ei = pr * ai + pi * ar
-        left = dot(table_a[...], jnp.concatenate([er.astype(bf), ei.astype(bf)], 0)).astype(bf)
-        far = dot(jnp.concatenate([left[:m], left[m:]], 1), table_b[...])
-        fr, fi = far[:, :m], far[:, m:]
-        ratio = amplitudes[j].astype(jnp.float32) / jnp.maximum(jnp.sqrt(fr * fr + fi * fi), 0.2)
-        projected = jnp.concatenate([(fr * ratio).astype(bf), (fi * ratio).astype(bf)], 0)
-        back_half = dot(table_b[...], projected).astype(bf)
-        back = dot(jnp.concatenate([back_half[:m], back_half[m:]], 1), table_a[...])
-        dr = back[:, :m] - er
-        di = back[:, m:] - ei
-        tr = ar * dr + ai * di
-        ti = ar * di - ai * dr
-        sum_r = tr if sum_r is None else sum_r + tr
-        sum_i = ti if sum_i is None else sum_i + ti
-        place(j, 0, pr * dr + pi * di)
-        place(j, 1, pr * di - pi * dr)
-    n, s, lanes = prob.shape[1:]
-    for k, value in enumerate((sum_r, sum_i)):
-        for c in range(n):
-            r0, l0 = c * s % m, c * s // m * lanes
-            prob[k, c] = value[r0 : r0 + s, l0 : l0 + lanes]
-
-
-def reduce_kernel(nx, ny, *refs):
-    grad, prob, core, icore, total = refs[:5]
-    (pair, acc, xr1, xr2, zr1, zr2, ipair, iacc, ixr1, ixr2, izr1, izr2) = refs[5:17]
-    (ppair, pacc, p1, pr1, pr2) = refs[17:22]
-    (gsend, grecv, isend, irecv, psend, precv) = refs[22:]
-    p = lax.axis_index("pos")
-    partner = {"pos": 1 - p}
-    line_greet(nx, ny, partner)
-    roles = [Role(q, nx, ny) for q in range(2)]
+    halos = [Halo(r, spec, pad, hsend, hrecv, partner) for r in roles]
     folds = [
-        Fold(r, grad.at[r.q], grad.at[r.o], pair, acc, (xr1, xr2, zr1, zr2), core, gsend, grecv, partner)
+        Fold(r, grad.at[r.q], grad.at[r.o], pair, acc, (xr1, xr2, zr1, zr2), None, gsend, grecv, partner)
         for r in roles
     ]
     lights = [
@@ -504,7 +486,7 @@
             ipair,
             iacc,
             (ixr1, ixr2, izr1, izr2),
-            icore,
+            light_all,
             isend,
             irecv,
             partner,
@@ -515,57 +497,115 @@
         ProbeSum(r, prob.at[r.q], prob.at[r.o], ppair, pacc, p1, pr1, pr2, total, psend, precv, partner)
         for r in roles
     ]
+    placer = Placer(offsets, bufs, m, positions)
+
+    def gather(k):
+        for g in range(4):
+            for b in range(2):
+                grad[k, g, b] = placer.rows(k, (2 * g + b) * h, h)
+
+    each(lambda q: halos[q].begin())
+    for i, at in enumerate(
+        (
+            (slice(None), pl.ds(0, half // 8)),
+            (slice(None), pl.ds((half + tile) // 8, half // 8)),
+            (slice(None), slice(None), slice(None), pl.ds(0, half)),
+            (slice(None), slice(None), slice(None), pl.ds(half + tile, half)),
+        )
+    ):
+
+        @pl.when(jnp.logical_not(sides[i].has))
+        def _(at=at):
+            pad[at] = jnp.zeros(pad.at[at].shape, pad.dtype)
+
+    placer.clear()
+    loads[1].wait()
+    power = probe[0] * probe[0] + probe[1] * probe[1]
+    for j in range(positions):
+        placer.put(j, 2, power)
+    gather(2)
+    each(lambda q: lights[q].begin())
+
+    def rest(q):
+        halos[q].relay()
+        halos[1 - q].arrive()
+        lights[q].add(0)
+        lights[q].add(1)
+        lights[q].send_rims(0)
+        lights[q].add(2)
+
+    each(rest)
+    for c in loads[:1] + loads[2:]:
+        c.wait()
+    sums = [None, None]
+    for j in range(positions):
+        ar, ai = placer.window(j, pad, 0), placer.window(j, pad, 1)
+        pr, pi = probe[0], probe[1]
+        dr, di = project((ar, ai), pr, pi, amplitudes[j], table_a, table_b)
+        for k, t in enumerate((ar * dr + ai * di, ar * di - ai * dr)):
+            sums[k] = t if sums[k] is None else sums[k] + t
+        placer.put(j, 0, pr * dr + pi * di)
+        placer.put(j, 1, pr * di - pi * dr)
+        if j == 0:
+
+            def light_mid(q):
+                lights[q].fold(0)
+                lights[q].send_rims(1)
+
+            each(light_mid)
+    n, s, lanes = prob.shape[1:]
+    for k in range(2):
+        for c in range(n):
+            r0, l0 = c * s % m, c * s // m * lanes
+            prob[k, c] = sums[k][r0 : r0 + s, l0 : l0 + lanes]
+    each(lambda q: probes[q].begin())
+    gather(0)
+    gather(1)
+
+    def update(q):
+        q4 = folds[q].q4
+        for g in range(2):
+            for b in range(2):
+                r0 = (2 * g + b) * h
+                old = pad[q, (half + r0) // 8 : (half + r0 + h) // 8, :, half : half + tile].reshape(h, tile)
+                new_spec[q, r0 : r0 + h] = old + acc[1 + g, b, :, q4 : 3 * q4] / (light_all[b, g, 0] + 1.0)
+
+    def share_copy(q):
+        return remote(new_spec.at[q], new_spec.at[q], gsend.at[7], grecv.at[7], partner)
 
     def objects(q):
         probe_sum, fold, light = probes[q], folds[q], lights[q]
-        probe_sum.begin()
         fold.begin()
-        light.begin()
+        light.fold(1)
+        light.share()
         probe_sum.step1()
         fold.add(0)
         fold.add(1)
         fold.send_rims(0)
-        light.add(0)
-        light.add(1)
-        light.send_rims(0)
         fold.add(2)
-        light.add(2)
         probe_sum.step2()
         fold.fold(0)
         fold.send_rims(1)
-        light.fold(0)
-        light.send_rims(1)
         probe_sum.step3()
+        light.arrive()
         fold.fold(1)
-        fold.share()
-        light.fold(1)
-        light.share()
+        update(q)
+        share_copy(q).start()
         probe_sum.step4()
-        light.arrive()
-        fold.arrive()
 
     each(objects)
+
     def closing(q):
         probes[q].step5()
         probes[1 - q].arrive()
+        share_copy(1 - q).wait_recv()
+        share_copy(q).wait_send()
         lights[q].finish()
         folds[q].finish()
         probes[q].finish()
+        halos[q].finish()
 
     each(closing)
-
-def apply_kernel(step_size, core, light, total, pad, probe, new_spec, new_probe):
-    tile = new_spec.shape[1]
-    half = (pad.shape[1] - tile) // 2
-    m = probe.shape[1]
-    h = core.shape[3]
-    for k in range(2):
-        for g in range(2):
-            for b in range(2):
-                r0 = (2 * g + b) * h
-                old = pad[k, half + r0 : half + r0 + h, half : half + tile]
-                new_spec[k, r0 : r0 + h] = old + core[k, g, b] / (light[b, g, 0] + 1.0)
-    n, s, lanes = total.shape[1:]
     for k in range(2):
         for c in range(n):
             rows = slice(c * s % m, c * s % m + s)
@@ -591,7 +631,7 @@
     f32 = jnp.float32
     vm = pl.BlockSpec(memory_space=VMEM)
     sm = pl.BlockSpec(memory_space=pltpu.SMEM)
-    anywhere = pl.BlockSpec(memory_space=pl.ANY)
+    hbm = pl.BlockSpec(memory_space=pltpu.HBM)
     dma = pltpu.SemaphoreType.DMA
     lanes = 128
     n = nx * ny
@@ -599,29 +639,7 @@
     h = wide // 8
     most = max(nx, ny)
     positions = offsets.shape[0]
-    shaped = VMEM
-    held = (offsets, probe_wave, amplitudes, consts[0], consts[1])
-    hbm = pl.BlockSpec(memory_space=pltpu.HBM)
-    pad, *held = pl.pallas_call(
-        functools.partial(halo_kernel, nx, ny),
-        out_shape=[shaped((2, wide, wide), f32)] + [shaped(x.shape, x.dtype) for x in held],
-        in_specs=[hbm] * 6,
-        out_specs=[vm] * 6,
-        scratch_shapes=[dma((16,)), dma((16,)), dma((6,))],
-        compiler_params=pltpu.CompilerParams(vmem_limit_bytes=16 * 2**20, collective_id=0, has_side_effects=True),
-        name="halo",
-    )(*[pltpu.with_memory_space_constraint(x, pltpu.HBM) for x in (specimen, *held)])
-    grad, prob = pl.pallas_call(
-        step_kernel,
-        out_shape=[
-            jax.ShapeDtypeStruct((3, wide, wide), f32),
-            jax.ShapeDtypeStruct((2, n, s, lanes), f32),
-        ],
-        in_specs=[sm] + [vm] * 5,
-        out_specs=[vm, vm],
-        compiler_params=pltpu.CompilerParams(vmem_limit_bytes=32 * 2**20),
-        name="step",
-    )(held[0], pad, *held[1:])
+    held = (probe_wave, amplitudes, consts[0], consts[1])
 
     def field(size):
         return [
@@ -634,16 +652,19 @@
         ]
 
     step_size = 1.0 / math.sqrt(positions * n * 2)
-    core, light, total = pl.pallas_call(
-        functools.partial(reduce_kernel, nx, ny),
-        out_shape=[
-            shaped((2, 2, 2, h, wide // 2), f32),
-            shaped((2, 2, 1, h, wide // 2), f32),
-            shaped((2, n, s, lanes), f32),
-        ],
-        in_specs=[vm] * 2,
-        out_specs=[vm, vm, vm],
+    return pl.pallas_call(
+        functools.partial(whole_kernel, nx, ny, step_size),
+        out_shape=[VMEM(specimen.shape, f32), VMEM(probe_wave.shape, f32)],
+        in_specs=[sm] + [hbm] * 5,
+        out_specs=[vm, vm],
         scratch_shapes=[
+            VMEM((2, wide // 8, 8, wide), f32),
+            *[VMEM(x.shape, x.dtype) for x in held],
+            VMEM((positions, 3, (2 * (tile - 8) + m + 8) // 8, 8, wide), f32),
+            VMEM((3, 4, 2, h, wide), f32),
+            VMEM((2, n, s, lanes), f32),
+            VMEM((2, n, s, lanes), f32),
+            VMEM((2, 2, 1, h, wide // 2), f32),
             *field(2),
             *field(1),
             VMEM((n, s, lanes), f32),
@@ -651,6 +672,9 @@
             VMEM((most, s, lanes), f32),
             VMEM((n, s, lanes), f32),
             VMEM((most, s, lanes), f32),
+            dma((16,)),
+            dma((16,)),
+            dma((5,)),
             dma((8,)),
             dma((8,)),
             dma((8,)),
@@ -658,20 +682,9 @@
             dma((6, most)),
             dma((6, most)),
         ],
-        compiler_params=pltpu.CompilerParams(vmem_limit_bytes=32 * 2**20, collective_id=1, has_side_effects=True),
-        name="reduce",
-    )(grad.reshape(3, 4, 2, h, wide), prob)
-    return pl.pallas_call(
-        functools.partial(apply_kernel, step_size),
-        out_shape=[
-            jax.ShapeDtypeStruct(specimen.shape, f32),
-            jax.ShapeDtypeStruct(probe_wave.shape, f32),
-        ],
-        in_specs=[vm] * 5,
-        out_specs=[vm, vm],
-        compiler_params=pltpu.CompilerParams(vmem_limit_bytes=16 * 2**20),
-        name="apply",
-    )(core, light, total, pad, held[1])
+        compiler_params=pltpu.CompilerParams(vmem_limit_bytes=56 * 2**20, collective_id=0, has_side_effects=True),
+        name="whole",
+    )(offsets, *[pltpu.with_memory_space_constraint(x, pltpu.HBM) for x in (specimen.reshape(2, tile // 8, 8, tile), *held)])
 
 
 def solution(mesh):

time: 42.6 us -> 43.2 us (1.014)
  local copies, waits for them, and re-layouts: 0 us -> 1.59 us
  Pallas kernels: 41.8 us -> 40.8 us
    unnamed x0 -> x2, local copies, waits for them, and re-layouts: none -> 1.59 us
    pallas_call x4 -> x1, Pallas kernels: 41.8 us -> 40.8 us  [shards(): pl.pallas_call(functools.partial(whole_kernel, nx, ny, step_size), out_sh...]
where the time goes in v1:
time: 43.2 us; the launch traced here: 43 us
  Pallas kernels  40.8 us (94%)
  local copies, waits for them, and re-layouts  1.59 us (4%)
  between operations  0.64 us (1%)
    pallas_call x1, Pallas kernels, shards(): pl.pallas_call(functools.partial(whole_kernel, nx, ny, step_size), out_sh...  40.8 us
    unnamed x2, local copies, waits for them, and re-layouts  1.59 us

profile of v1, /device:TPU:0, one launch (start us, length us, event | category | flops | bytes accessed | tf_op | source)
XLA Modules:
  0.0 43.0 jit_solution(397598376973741142)
XLA Ops:
  0.6 40.8 %whole.1 = (f32[2,256,256]{2,1,0:T(8,128)S(1)}, f32[2,256,256]{2,1,0:T(8,128)S(1)}) custom-call(s32[2,2]{1,0:T(2,128)} %refs_0_.1, f32[2,32,8,256]{3,2,1,0:T(8,128)} %bitcast.1, f32[2,256,256]{2,1,0:T(8,128)} %refs_2_.1, bf16[2,256,256]{2,1,0:T(8,128)(2,1)} %refs_3_.1, bf16[512,512]{1,0:T(8,128)(2,1)} %constant.4.clone.refs_4_, ...), custom_call_target="tpu_custom_call" | custom-call | tf_op jit(solution)/shard_map/whole/pallas_call | solution.py:655
  41.4 0.8 %copy.10 = f32[2,256,256]{2,1,0:T(8,128)} copy(f32[2,256,256]{2,1,0:T(8,128)S(1)} %get-tuple-element.2) | data formatting | bytes 1048576
  42.2 0.8 %copy.11 = f32[2,256,256]{2,1,0:T(8,128)} copy(f32[2,256,256]{2,1,0:T(8,128)S(1)} %get-tuple-element.3) | data formatting | bytes 1048576

commit v2 on v1

v2 whole, which is shorter than its diff:
```python
import functools
import math

import jax
import jax.numpy as jnp
import numpy as np
from jax import lax
from jax.experimental import pallas as pl
from jax.experimental.pallas import tpu as pltpu
from jax.sharding import PartitionSpec as P

MESH = pl.DeviceIdType.MESH
VMEM = pltpu.VMEM


def remote(src, dst, send, recv, where):
    return pltpu.make_async_remote_copy(
        src_ref=src, dst_ref=dst, send_sem=send, recv_sem=recv, device_id=where, device_id_type=MESH
    )


def greet(conditions_devices):
    barrier = pltpu.get_barrier_semaphore()
    for present, where in conditions_devices:
        if present is True:
            pl.semaphore_signal(barrier, inc=1, device_id=where, device_id_type=MESH)
        else:

            @pl.when(present)
            def _(where=where):
                pl.semaphore_signal(barrier, inc=1, device_id=where, device_id_type=MESH)

    fixed = sum(1 for present, _ in conditions_devices if present is True)
    peers = [present.astype(jnp.int32) for present, _ in conditions_devices if present is not True]
    pl.semaphore_wait(barrier, sum(peers, fixed))


class Side:
    def __init__(self, axis, count, step):
        me = lax.axis_index(axis)
        self.has = me > 0 if step < 0 else me < count - 1
        self.where = {axis: me + step}


class Role:
    def __init__(self, q, nx, ny, order=None):
        order = q if order is None else order
        along_x = ("scanx", nx, Side("scanx", nx, -1), Side("scanx", nx, 1))
        along_y = ("scany", ny, Side("scany", ny, -1), Side("scany", ny, 1))
        one, two = (along_y, along_x) if order == 0 else (along_x, along_y)
        self.q, self.o, self.rows_first = q, 1 - q, order == 1
        self.axis1, self.n1, self.sides1 = one[0], one[1], one[2:]
        self.axis2, self.n2, self.sides2 = two[0], two[1], two[2:]
        self.me1, self.me2 = lax.axis_index(self.axis1), lax.axis_index(self.axis2)


def when(*conditions):
    return pl.when(functools.reduce(jnp.logical_and, conditions))


def dot(a, b):
    return jnp.dot(a, b, preferred_element_type=jnp.float32)


class Halo:
    def __init__(self, role, spec, pad, send, recv, partner):
        self.r, self.spec, self.pad, self.partner = role, spec, pad, partner
        self.send, self.recv = send, recv
        tile = spec.shape[3]
        half = (pad.shape[3] - tile) // 2
        self.own = (half, tile)
        self.margins = ((0, half), (half + tile, half))
        self.edges = ((0, half), (tile - half, half))
        self.pad_edges = ((half, half), (tile, half))
        self.whole = (0, tile)

    def at(self, one, two):
        rows, cols = (one, two) if self.r.rows_first else (two, one)
        return (self.r.q, pl.ds(rows[0] // 8, rows[1] // 8), slice(None), pl.ds(*cols))

    def copy(self, src, dst, i, where):
        return remote(src, dst, self.send.at[i], self.recv.at[i], where)

    def strip1(self, m, e):
        return self.copy(
            self.spec.at[self.at(self.edges[1 - m], self.edges[e])],
            self.pad.at[self.at(self.margins[m], self.pad_edges[e])],
            2 * m + e,
            self.r.sides1[1 - m].where,
        )

    def strip2(self, m):
        return self.copy(
            self.spec.at[self.at(self.whole, self.edges[1 - m])],
            self.pad.at[self.at(self.own, self.margins[m])],
            4 + m,
            self.r.sides2[1 - m].where,
        )

    def corner(self, m1, m2):
        return self.copy(
            self.pad.at[self.at(self.margins[m1], self.pad_edges[1 - m2])],
            self.pad.at[self.at(self.margins[m1], self.margins[m2])],
            6 + 2 * m1 + m2,
            self.r.sides2[1 - m2].where,
        )

    def share(self, i, one, two):
        ref = self.pad.at[self.at(one, two)]
        return self.copy(ref, ref, 10 + i, self.partner)

    def share1(self, m, e):
        return self.share(2 * m + e, self.margins[m], self.pad_edges[e])

    def share2(self, m):
        return self.share(4 + m, self.own, self.margins[m])

    def share_corner(self, m1, m2):
        return self.share(6 + 2 * m1 + m2, self.margins[m1], self.margins[m2])

    def begin(self):
        r = self.r
        for m in range(2):
            for e in range(2):
                when(r.sides1[1 - m].has, r.sides2[e].has)(self.strip1(m, e).start)
        for m in range(2):
            when(r.sides2[1 - m].has)(self.strip2(m).start)
        for m in range(2):
            for e in range(2):
                when(r.sides1[1 - m].has, jnp.logical_not(r.sides2[e].has))(self.strip1(m, e).start)

    def relay(self):
        r = self.r
        for m1 in range(2):
            for e in range(2):

                @when(r.sides1[m1].has, r.sides2[e].has)
                def _():
                    self.strip1(m1, e).wait_recv()
                    self.corner(m1, 1 - e).start()
                    self.share1(m1, e).start()

        for m in range(2):

            @when(r.sides2[m].has)
            def _():
                self.strip2(m).wait_recv()
                self.share2(m).start()

        for m1 in range(2):
            for e in range(2):

                @when(r.sides1[m1].has, jnp.logical_not(r.sides2[e].has))
                def _():
                    self.strip1(m1, e).wait_recv()
                    self.share1(m1, e).start()

    def relay_corners(self):
        r = self.r
        for m1 in range(2):
            for m2 in range(2):

                @when(r.sides1[m1].has, r.sides2[m2].has)
                def _():
                    self.corner(m1, m2).wait_recv()
                    self.share_corner(m1, m2).start()

    def arrive(self):
        r = self.r
        for m in range(2):
            for e in range(2):
                when(r.sides1[m].has)(self.share1(m, e).wait_recv)
            when(r.sides2[m].has)(self.share2(m).wait_recv)
        for m1 in range(2):
            for m2 in range(2):
                when(r.sides1[m1].has, r.sides2[m2].has)(self.share_corner(m1, m2).wait_recv)

    def finish(self):
        r = self.r
        for m in range(2):
            for e in range(2):
                when(r.sides1[1 - m].has)(self.strip1(m, e).wait_send)
                when(r.sides1[m].has)(self.share1(m, e).wait_send)
            when(r.sides2[1 - m].has)(self.strip2(m).wait_send)
            when(r.sides2[m].has)(self.share2(m).wait_send)
        for m1 in range(2):
            for m2 in range(2):
                when(r.sides1[m1].has, r.sides2[1 - m2].has)(self.corner(m1, m2).wait_send)
                when(r.sides1[m1].has, r.sides2[m2].has)(self.share_corner(m1, m2).wait_send)


class Fold:
    def __init__(self, role, mine, theirs, pair, acc, rims, core, send, recv, partner):
        self.r, self.mine, self.theirs, self.pair, self.acc = role, mine, theirs, pair, acc
        self.rims = rims
        self.core, self.send, self.recv, self.partner = core, send, recv, partner
        w = acc.shape[-1]
        self.w, self.q4 = w, w // 4

    def piece(self, i):
        q4, cols = self.q4, (slice(None),) * 3
        if self.r.rows_first:
            return ((pl.ds(0, 1),), (pl.ds(3, 1),), (pl.ds(1, 2),))[i]
        return cols + ((pl.ds(0, q4),), (pl.ds(3 * q4, q4),), (pl.ds(q4, 2 * q4),))[i]

    def needed(self, i):
        return pl.when(self.r.sides1[i].has) if i < 2 else lambda f: f()

    def pair_copy(self, i):
        at = self.piece(i)
        return remote(self.theirs.at[at], self.pair.at[at], self.send.at[i], self.recv.at[i], self.partner)

    def begin(self):
        for i in range(3):
            self.needed(i)(self.pair_copy(i).start)

    def add(self, i):
        @self.needed(i)
        def _():
            self.pair_copy(i).wait_recv()
            at = self.piece(i)
            self.acc[at] = self.mine[at] + self.pair[at]

    def rim_copy(self, stage, m):
        r, q4, w = self.r, self.q4, self.w
        rows = r.rows_first == (stage == 0)
        k = 1 - m
        if rows:
            cols = pl.ds(0, w) if stage == 0 else pl.ds(q4, 2 * q4)
            src = self.acc.at[3 * k, :, :, cols]
        else:
            groups = pl.ds(0, 4) if stage == 0 else pl.ds(1, 2)
            src = self.acc.at[groups, :, :, pl.ds(3 * k * q4, q4)]
        rim = self.rims[stage]
        sides = r.sides1 if stage == 0 else r.sides2
        i = 3 + 2 * stage + m
        return remote(src, rim.at[m], self.send.at[i], self.recv.at[i], sides[k].where)

    def send_rims(self, stage):
        sides = self.r.sides1 if stage == 0 else self.r.sides2
        for m in range(2):
            when(sides[1 - m].has)(self.rim_copy(stage, m).start)

    def fold(self, stage):
        r, q4, w, acc = self.r, self.q4, self.w, self.acc
        rows = r.rows_first == (stage == 0)
        sides = r.sides1 if stage == 0 else r.sides2
        for m in range(2):

            @when(sides[m].has)
            def _():
                self.rim_copy(stage, m).wait_recv()
                if rows:
                    cols = pl.ds(0, w) if stage == 0 else pl.ds(q4, 2 * q4)
                    rim = self.rims[stage]
                    acc[1 + m, :, :, cols] = acc[1 + m, :, :, cols] + rim[m]
                else:
                    groups = pl.ds(0, 4) if stage == 0 else pl.ds(1, 2)
                    cols = pl.ds((1 + m) * q4, q4)
                    rim = self.rims[stage]
                    acc[groups, :, :, cols] = acc[groups, :, :, cols] + rim[m]

    def share_copy(self, q):
        return remote(self.core.at[q], self.core.at[q], self.send.at[7], self.recv.at[7], self.partner)

    def share(self):
        q4 = self.q4
        self.core[self.r.q] = self.acc[1:3, :, :, q4 : 3 * q4]
        self.share_copy(self.r.q).start()

    def arrive(self):
        self.share_copy(self.r.o).wait_recv()

    def finish(self):
        r = self.r
        for i in range(3):
            self.needed(i)(self.pair_copy(i).wait_send)
        for m in range(2):
            when(r.sides1[1 - m].has)(self.rim_copy(0, m).wait_send)
            when(r.sides2[1 - m].has)(self.rim_copy(1, m).wait_send)
        if self.core is not None:
            self.share_copy(r.q).wait_send()


class ProbeSum:
    def __init__(self, q, nx, ny, prob, ppair, held, inner, hub, part, total, send, recv, partner):
        self.q, self.ny = q, ny
        self.prob, self.ppair, self.held = prob, ppair, held
        self.inner, self.hub, self.part, self.total = inner, hub, part, total
        self.send, self.recv, self.partner = send, recv, partner
        self.chunks = send.shape[1]
        self.rows = prob.shape[1] // self.chunks
        me, mid = lax.axis_index("scanx"), nx // 2
        step = 2 * (me < mid).astype(jnp.int32) - 1
        self.to_inner, self.to_outer = {"scanx": me + step}, {"scanx": me - step}
        self.has_outer = jnp.logical_and(me > 0, me < nx - 1)
        self.no_outer = jnp.logical_not(self.has_outer)
        self.is_hub = jnp.logical_or(me == mid - 1, me == mid)
        self.not_hub = jnp.logical_not(self.is_hub)
        self.mine = lax.axis_index("scany")

    def at(self, c):
        return pl.ds(c * self.rows, self.rows)

    def copy(self, src, dst, s, r, c, where):
        return remote(src.at[self.at(c)], dst.at[self.at(c)], self.send.at[s, c], self.recv.at[r, c], where)

    def pair(self, c):
        return self.copy(self.prob.at[1 - self.q], self.ppair, 0, 0, c, self.partner)

    def inward(self, c):
        return self.copy(self.part, self.inner, 1, 1, c, self.to_inner)

    def across(self, c):
        return self.copy(self.part, self.hub, 1, 2, c, self.to_inner)

    def outward(self, c, src):
        return self.copy(src, self.hub, 2, 2, c, self.to_outer)

    def share(self, c, q):
        return self.copy(self.total.at[q], self.total.at[q], 3, 3, c, self.partner)

    def sides(self, c):
        out = []
        for d in range(1, self.ny):
            slot = self.held.at[self.mine]
            out.append(self.copy(slot, slot, 3 + d, 3 + d, c, {"scany": lax.rem(self.mine + d, self.ny)}))
        return out

    def side_arrive(self, c):
        for d in range(1, self.ny):
            slot = self.held.at[lax.rem(self.mine - d + self.ny, self.ny)]
            self.copy(slot, slot, 3 + d, 3 + d, c, self.partner).wait_recv()

    def side_sum(self, c):
        self.side_arrive(c)
        out = self.held[0, self.at(c)]
        for i in range(1, self.ny):
            out = out + self.held[i, self.at(c)]
        return out

    def pair_sum(self, c):
        self.pair(c).wait_recv()
        return self.prob[self.q, self.at(c)] + self.ppair[self.at(c)]

    def send_sides(self, c, value):
        self.held[self.mine, self.at(c)] = value
        for copy in self.sides(c):
            copy.start()

    def send_inward(self, c):
        when(self.not_hub)(self.inward(c).start)
        when(self.is_hub)(self.across(c).start)

    def collect(self):
        @pl.when(self.has_outer)
        def _():
            for c in range(self.chunks):
                self.inward(c).wait_recv()
                self.part[self.at(c)] = self.part[self.at(c)] + self.inner[self.at(c)]
                self.send_inward(c)

    def start_part(self, c, value):
        self.part[self.at(c)] = value
        when(self.no_outer)(functools.partial(self.send_inward, c))

    def from_hub(self, hubs, after, chunks=None):
        @pl.when(self.is_hub if hubs else self.not_hub)
        def _():
            for c in chunks or range(self.chunks):
                self.across(c).wait_recv()
                value = self.hub[self.at(c)]
                after(c, self.part[self.at(c)] + value if hubs else value)

    def finish(self, src):
        for c in range(self.chunks):
            self.pair(c).wait_send()
            self.inward(c).wait_send()
            when(self.has_outer)(self.outward(c, src).wait_send)
            self.share(c, self.q).wait_send()
            for copy in self.sides(c):
                copy.wait_send()


class SideFirst(ProbeSum):
    def one(self):
        for c in range(self.chunks):
            self.send_sides(c, self.pair_sum(c))

    def two(self):
        for c in range(self.chunks):
            self.start_part(c, self.side_sum(c))
        self.collect()

    def done(self, c, value):
        self.total[self.q, self.at(c)] = value
        when(self.has_outer)(self.outward(c, self.total.at[self.q]).start)
        self.share(c, self.q).start()

    def three(self, chunks=None):
        self.from_hub(True, self.done, chunks)

    def four(self):
        self.from_hub(False, self.done)

    def five(self):
        pass

    def end(self):
        self.finish(self.total.at[self.q])


class ChainFirst(ProbeSum):
    def one(self):
        for c in range(self.chunks):
            self.start_part(c, self.pair_sum(c))

    def two(self):
        self.collect()

    def done(self, c, value):
        self.send_sides(c, value)
        when(self.has_outer)(self.outward(c, self.held.at[self.mine]).start)

    def three(self, chunks=None):
        self.from_hub(True, self.done, chunks)

    def four(self):
        self.from_hub(False, self.done)

    def five(self):
        for c in range(self.chunks):
            self.total[self.q, self.at(c)] = self.side_sum(c)
            self.share(c, self.q).start()

    def end(self):
        self.finish(self.held.at[self.mine])


def near_greet(ny, partner, sides):
    my = lax.axis_index("scany")
    greet(
        [(True, partner)]
        + [(True, {"scany": lax.rem(my + d, ny)}) for d in range(1, ny)]
        + [(side.has, side.where) for side in sides]
    )


def each(step):
    p = lax.axis_index("pos")
    for q in range(2):
        pl.when(p == q)(functools.partial(step, q))


class Placer:
    def __init__(self, offsets, bufs, m, positions):
        self.bufs, self.m = bufs, m
        self.tall, self.span = m + 8, m + 128
        self.top = (bufs.shape[2] - self.tall // 8) // 2
        self.spots = []
        for j in range(positions):
            row, col = offsets[j, 0], offsets[j, 1]
            self.spots.append((lax.rem(row, 8), lax.rem(col, 128), lax.div(row, 8), lax.div(col, 128)))

    def clear(self):
        n, k, rows = self.bufs.shape[:3]
        bottom = self.top + self.tall // 8
        for j in range(n):
            for c in range(k):
                self.bufs[j, c, 0 : self.top] = jnp.zeros((self.top, *self.bufs.shape[3:]), jnp.float32)
                self.bufs[j, c, bottom:rows] = jnp.zeros((rows - bottom, *self.bufs.shape[3:]), jnp.float32)

    def put(self, j, k, term):
        row_in, col_in, _, step = self.spots[j]
        m, wide = self.m, self.bufs.shape[4]
        blank_rows = jnp.zeros((self.tall - m, m), jnp.float32)
        blank_cols = jnp.zeros((self.tall, self.span - m), jnp.float32)
        moved = pltpu.roll(jnp.concatenate([term, blank_rows], 0), row_in, 0)
        moved = pltpu.roll(jnp.concatenate([moved, blank_cols], 1), col_in, 1)
        out = None
        for d in range((wide - self.span) // 128 + 1):
            parts = [jnp.zeros((self.tall, w), jnp.float32) for w in (128 * d, wide - self.span - 128 * d)]
            here = jnp.concatenate([x for x in (parts[0], moved, parts[1]) if x.shape[1]], 1)
            out = here if out is None else jnp.where(step == d, here, out)
        self.bufs[j, k, self.top : self.top + self.tall // 8] = out.reshape(self.tall // 8, 8, wide)

    def rows(self, k, r0, count):
        out = None
        for j, (_, _, row, _) in enumerate(self.spots):
            part = self.bufs[j, k, pl.ds(self.top - row + r0 // 8, count // 8)]
            out = part if out is None else out + part
        return out.reshape(count, self.bufs.shape[4])

    def window(self, j, pad, k):
        row_in, col_in, row, step = self.spots[j]
        wide = pad.shape[3]
        block = pad[k, pl.ds(row, self.tall // 8)].reshape(self.tall, wide)
        out = block[:, : self.span]
        for d in range(1, (wide - self.span) // 128 + 1):
            out = jnp.where(step == d, block[:, 128 * d : 128 * d + self.span], out)
        out = pltpu.roll(out, lax.rem(self.span - col_in, self.span), 1)[:, : self.m]
        return pltpu.roll(out, lax.rem(self.tall - row_in, self.tall), 0)[: self.m]


def forward(window, pr, pi, table_a, table_b):
    m = pr.shape[0]
    bf = jnp.bfloat16
    ar, ai = window
    er = pr * ar - pi * ai
    ei = pr * ai + pi * ar
    left = dot(table_a[...], jnp.concatenate([er.astype(bf), ei.astype(bf)], 0)).astype(bf)
    return er, ei, dot(jnp.concatenate([left[:m], left[m:]], 1), table_b[...])


def backward(er, ei, far, amplitude, table_a, table_b):
    m = er.shape[0]
    bf = jnp.bfloat16
    fr, fi = far[:, :m], far[:, m:]
    ratio = amplitude.astype(jnp.float32) / jnp.maximum(jnp.sqrt(fr * fr + fi * fi), 0.2)
    projected = jnp.concatenate([(fr * ratio).astype(bf), (fi * ratio).astype(bf)], 0)
    back_half = dot(table_b[...], projected).astype(bf)
    back = dot(jnp.concatenate([back_half[:m], back_half[m:]], 1), table_a[...])
    return back[:, :m] - er, back[:, m:] - ei


def whole_kernel(nx, ny, step_size, *refs):
    offsets, spec, *given = refs[:6]
    new_spec, new_probe = refs[6:8]
    pad, probe, amplitudes, table_a, table_b, bufs, grad, prob, total, light_all = refs[8:18]
    pair, acc, xr, zr, ipair, iacc, ixr, izr, ppair, held, inner, hub, part = refs[18:31]
    hsend, hrecv, local, gsend, grecv, isend, irecv, psend, precv = refs[31:]
    tile, m = spec.shape[3], probe.shape[1]
    wide = pad.shape[3]
    half = (wide - tile) // 2
    h = grad.shape[3]
    positions, chunks = amplitudes.shape[0], psend.shape[1]
    p = lax.axis_index("pos")
    partner = {"pos": 1 - p}
    loads = [pltpu.make_async_copy(spec, pad.at[:, pl.ds(half // 8, tile // 8), :, pl.ds(half, tile)], local.at[0])]
    for i, (src, dst) in enumerate(zip(given, (probe, amplitudes, table_a, table_b)), 1):
        loads.append(pltpu.make_async_copy(src, dst, local.at[i]))
    for c in loads:
        c.start()
    roles = [Role(q, nx, ny) for q in range(2)]
    sides = roles[1].sides1 + roles[0].sides1
    near_greet(ny, partner, roles[1].sides1)
    halos = [Halo(r, spec, pad, hsend, hrecv, partner) for r in roles]
    role = Role(p, nx, ny, 0)
    fold = Fold(role, grad.at[p], grad.at[1 - p], pair, acc, (xr, zr), None, gsend, grecv, partner)
    light = Fold(
        role,
        grad.at[2, :, pl.ds(p, 1)],
        grad.at[2, :, pl.ds(1 - p, 1)],
        ipair,
        iacc,
        (ixr, izr),
        light_all,
        isend,
        irecv,
        partner,
    )
    probes = [
        kind(q, nx, ny, prob, ppair, held, inner, hub, part, total, psend, precv, partner)
        for q, kind in enumerate((SideFirst, ChainFirst))
    ]
    placer = Placer(offsets, bufs, m, positions)

    def gather(k):
        for g in range(4):
            for b in range(2):
                grad[k, g, b] = placer.rows(k, (2 * g + b) * h, h)

    each(lambda q: halos[q].begin())
    for i, at in enumerate(
        (
            (slice(None), pl.ds(0, half // 8)),
            (slice(None), pl.ds((half + tile) // 8, half // 8)),
            (slice(None), slice(None), slice(None), pl.ds(0, half)),
            (slice(None), slice(None), slice(None), pl.ds(half + tile, half)),
        )
    ):

        @pl.when(jnp.logical_not(sides[i].has))
        def _(at=at):
            pad[at] = jnp.zeros(pad.at[at].shape, pad.dtype)

    placer.clear()
    loads[1].wait()
    power = probe[0] * probe[0] + probe[1] * probe[1]
    for j in range(positions):
        placer.put(j, 2, power)
    gather(2)
    light.begin()

    def strips(q):
        halos[q].relay()

    def corners(q):
        halos[q].relay_corners()
        halos[1 - q].arrive()

    each(strips)
    for i in range(3):
        light.add(i)
    light.send_rims(0)
    each(corners)
    for c in loads[:1] + loads[2:]:
        c.wait()
    pr, pi = probe[0], probe[1]
    windows = [[placer.window(j, pad, k) for k in range(2)] for j in range(positions)]
    fields = [forward(windows[j], pr, pi, table_a, table_b) for j in range(positions)]
    light.fold(0)
    light.send_rims(1)
    diffs = [backward(*fields[j], amplitudes[j], table_a, table_b) for j in range(positions)]
    sums = [None, None]
    for (ar, ai), (dr, di) in zip(windows, diffs):
        for k, t in enumerate((ar * dr + ai * di, ar * di - ai * dr)):
            sums[k] = t if sums[k] is None else sums[k] + t
    rows = m // chunks
    for c in range(chunks):
        at = pl.ds(c * rows, rows)
        for k in range(2):
            prob[k, at] = sums[k][c * rows : (c + 1) * rows]
        remote(prob.at[1 - p, at], ppair.at[at], psend.at[0, c], precv.at[0, c], partner).start()
    for j, (dr, di) in enumerate(diffs):
        placer.put(j, 0, pr * dr + pi * di)
        placer.put(j, 1, pr * di - pi * dr)
    gather(1 - p)
    fold.begin()
    gather(p)

    def update(q):
        q4 = fold.q4
        for g in range(2):
            for b in range(2):
                r0 = (2 * g + b) * h
                old = pad[q, (half + r0) // 8 : (half + r0 + h) // 8, :, half : half + tile].reshape(h, tile)
                new_spec[q, r0 : r0 + h] = old + acc[1 + g, b, :, q4 : 3 * q4] / (light_all[b, g, 0] + 1.0)

    def share_copy(q):
        return remote(new_spec.at[q], new_spec.at[q], gsend.at[7], grecv.at[7], partner)

    def object_last(q):
        light.arrive()
        fold.fold(1)
        update(q)
        share_copy(q).start()

    def objects(q):
        probe_sum = probes[q]
        probe_sum.one()
        fold.add(0)
        fold.add(1)
        fold.send_rims(0)
        fold.add(2)
        light.fold(1)
        light.share()
        probe_sum.two()
        if q == 0:
            probe_sum.three(range(chunks // 2))
            fold.fold(0)
            fold.send_rims(1)
            probe_sum.three(range(chunks // 2, chunks))
            probe_sum.four()
            object_last(q)
        else:
            probe_sum.three()
            probe_sum.four()
            fold.fold(0)
            fold.send_rims(1)
            probe_sum.five()
            object_last(q)

    each(objects)

    def closing(q):
        for c in range(chunks):
            probes[q].share(c, 1 - q).wait_recv()
        share_copy(1 - q).wait_recv()
        share_copy(q).wait_send()
        light.finish()
        fold.finish()
        probes[q].end()
        halos[q].finish()

    each(closing)
    for k in range(2):
        new_probe[k] = probe[k] + total[k] * step_size


def emit_kernel(spec, probe, new_spec, new_probe, sem):
    copies = [
        pltpu.make_async_copy(src.at[k], dst.at[k], sem.at[i, k])
        for i, (src, dst) in enumerate(((spec, new_spec), (probe, new_probe)))
        for k in range(2)
    ]
    for c in copies:
        c.start()
    for c in copies:
        c.wait()


def tables(length):
    index = np.arange(length)
    angle = ((index[:, None] * index[None, :]) % length).astype(np.float32) * np.float32(2.0 * math.pi / length)
    scale = np.float32(1.0 / math.sqrt(length))
    c = np.cos(angle) * scale
    s = np.sin(angle) * scale
    a = np.block([[c, s], [-s, c]]).astype(jnp.bfloat16)
    b = np.block([[c, -s], [s, c]]).astype(jnp.bfloat16)
    return a, b


def shards(nx, ny, consts, specimen, probe_wave, amplitudes, offsets):
    m = probe_wave.shape[1]
    tile = specimen.shape[1]
    wide = tile + m
    f32 = jnp.float32
    vm = pl.BlockSpec(memory_space=VMEM)
    sm = pl.BlockSpec(memory_space=pltpu.SMEM)
    hbm = pl.BlockSpec(memory_space=pltpu.HBM)
    dma = pltpu.SemaphoreType.DMA
    n = nx * ny
    h = wide // 8
    chunks = 4
    positions = offsets.shape[0]
    held = (probe_wave, amplitudes, consts[0], consts[1])

    def field(size):
        return [
            VMEM((4, size, h, wide), f32),
            VMEM((4, size, h, wide), f32),
            VMEM((2, 4, size, h, wide // 4), f32),
            VMEM((2, size, h, wide // 2), f32),
        ]

    step_size = 1.0 / math.sqrt(positions * n * 2)
    results = pl.pallas_call(
        functools.partial(whole_kernel, nx, ny, step_size),
        out_shape=[VMEM(specimen.shape, f32), VMEM(probe_wave.shape, f32)],
        in_specs=[sm] + [hbm] * 5,
        out_specs=[vm, vm],
        scratch_shapes=[
            VMEM((2, wide // 8, 8, wide), f32),
            *[VMEM(x.shape, x.dtype) for x in held],
            VMEM((positions, 3, (2 * (tile - 8) + m + 8) // 8, 8, wide), f32),
            VMEM((3, 4, 2, h, wide), f32),
            VMEM((2, m, m), f32),
            VMEM((2, m, m), f32),
            VMEM((2, 2, 1, h, wide // 2), f32),
            *field(2),
            *field(1),
            VMEM((m, m), f32),
            VMEM((ny, m, m), f32),
            VMEM((m, m), f32),
            VMEM((m, m), f32),
            VMEM((m, m), f32),
            dma((20,)),
            dma((20,)),
            dma((5,)),
            dma((8,)),
            dma((8,)),
            dma((8,)),
            dma((8,)),
            dma((3 + ny, chunks)),
            dma((3 + ny, chunks)),
        ],
        compiler_params=pltpu.CompilerParams(vmem_limit_bytes=56 * 2**20, collective_id=0, has_side_effects=True),
        name="whole",
    )(offsets, *[pltpu.with_memory_space_constraint(x, pltpu.HBM) for x in (specimen.reshape(2, tile // 8, 8, tile), *held)])
    return pl.pallas_call(
        emit_kernel,
        out_shape=[jax.ShapeDtypeStruct(specimen.shape, f32), jax.ShapeDtypeStruct(probe_wave.shape, f32)],
        in_specs=[vm] * 2,
        out_specs=[pl.BlockSpec(memory_space=pl.ANY)] * 2,
        scratch_shapes=[dma((2, 2))],
        compiler_params=pltpu.CompilerParams(vmem_limit_bytes=2 * 2**20),
        name="emit",
    )(*results)


def solution(mesh):
    nx, ny = mesh.shape["scanx"], mesh.shape["scany"]

    def run(specimen, probe_wave, amplitudes, offsets):
        consts = tables(probe_wave.shape[2])
        return jax.shard_map(
            lambda *args: shards(nx, ny, [jnp.asarray(t) for t in consts], *args),
            mesh=mesh,
            in_specs=(
                P(None, ("groups", "scanx"), "scany"),
                P(None, "groups", None),
                P(("groups", "scanx", "scany", "pos"), None, None),
                P(("groups", "scanx", "scany", "pos"), None),
            ),
            out_specs=(P(None, ("groups", "scanx"), "scany"), P(None, "groups", None)),
            check_vma=False,
        )(specimen, probe_wave, amplitudes, offsets)

    return run
```

time: 43.2 us -> 41.2 us (0.954)
  local copies, waits for them, and re-layouts: 1.59 us -> 0 us
    unnamed x2 -> x0, local copies, waits for them, and re-layouts: 1.59 us -> none
    pallas_call x1, Pallas kernels: 40.8 us -> 39.4 us  [shards(): pl.pallas_call(functools.partial(whole_kernel, nx, ny, step_size), out_sh...]
    pallas_call x0 -> x1, Pallas kernels: none -> 1 us  [shards(): pl.pallas_call(emit_kernel, out_shape=[jax.ShapeDtypeStruct(specimen.shap...]
where the time goes in v2:
time: 41.2 us; the launch traced here: 41.1 us
  Pallas kernels  40.4 us (98%)
  between operations  0.64 us (2%)
    pallas_call x1, Pallas kernels, shards(): pl.pallas_call(functools.partial(whole_kernel, nx, ny, step_size), out_sh...  39.4 us
    pallas_call x1, Pallas kernels, shards(): pl.pallas_call(emit_kernel, out_shape=[jax.ShapeDtypeStruct(specimen.shap...  1 us

profile of v2, /device:TPU:0, one launch (start us, length us, event | category | flops | bytes accessed | tf_op | source)
XLA Modules:
  0.0 41.1 jit_solution(7352059117501135009)
XLA Ops:
  0.6 39.4 %whole.1 = (f32[2,256,256]{2,1,0:T(8,128)S(1)}, f32[2,256,256]{2,1,0:T(8,128)S(1)}) custom-call(s32[2,2]{1,0:T(2,128)} %refs_0_.1, f32[2,32,8,256]{3,2,1,0:T(8,128)} %bitcast.1, f32[2,256,256]{2,1,0:T(8,128)} %refs_2_.1, bf16[2,256,256]{2,1,0:T(8,128)(2,1)} %refs_3_.1, bf16[512,512]{1,0:T(8,128)(2,1)} %constant.4.clone.refs_4_, ...), custom_call_target="tpu_custom_call" | custom-call | tf_op jit(solution)/shard_map/whole/pallas_call | solution.py:738
  40.1 1.0 %emit.1 = (f32[2,256,256]{2,1,0:T(8,128)}, f32[2,256,256]{2,1,0:T(8,128)}) custom-call(f32[2,256,256]{2,1,0:T(8,128)S(1)} %get-tuple-element.4.spec, f32[2,256,256]{2,1,0:T(8,128)S(1)} %get-tuple-element.5.probe), custom_call_target="tpu_custom_call" | custom-call | tf_op jit(solution)/shard_map/emit/pallas_call | solution.py:771

commit v3 on v2

--- a/solution.py
+++ b/solution.py
@@ -190,51 +190,54 @@
 
 
 class Fold:
-    def __init__(self, role, mine, theirs, pair, acc, rims, core, send, recv, partner):
-        self.r, self.mine, self.theirs, self.pair, self.acc = role, mine, theirs, pair, acc
-        self.rims = rims
+    def __init__(self, role, other, mine, theirs, pair, acc, rims, core, send, recv, partner):
+        self.r, self.other, self.mine, self.theirs, self.pair, self.acc = role, other, mine, theirs, pair, acc
+        self.rows1, self.cols1, self.rows2, self.cols2 = rims
         self.core, self.send, self.recv, self.partner = core, send, recv, partner
         w = acc.shape[-1]
         self.w, self.q4 = w, w // 4
 
-    def piece(self, i):
+    def piece(self, i, r):
         q4, cols = self.q4, (slice(None),) * 3
-        if self.r.rows_first:
+        if r.rows_first:
             return ((pl.ds(0, 1),), (pl.ds(3, 1),), (pl.ds(1, 2),))[i]
         return cols + ((pl.ds(0, q4),), (pl.ds(3 * q4, q4),), (pl.ds(q4, 2 * q4),))[i]
 
-    def needed(self, i):
-        return pl.when(self.r.sides1[i].has) if i < 2 else lambda f: f()
-
-    def pair_copy(self, i):
-        at = self.piece(i)
+    def needed(self, i, r):
+        return pl.when(r.sides1[i].has) if i < 2 else lambda f: f()
+
+    def pair_copy(self, i, r):
+        at = self.piece(i, r)
         return remote(self.theirs.at[at], self.pair.at[at], self.send.at[i], self.recv.at[i], self.partner)
 
     def begin(self):
         for i in range(3):
-            self.needed(i)(self.pair_copy(i).start)
+            self.needed(i, self.other)(self.pair_copy(i, self.other).start)
 
     def add(self, i):
-        @self.needed(i)
+        @self.needed(i, self.r)
         def _():
-            self.pair_copy(i).wait_recv()
-            at = self.piece(i)
+            self.pair_copy(i, self.r).wait_recv()
+            at = self.piece(i, self.r)
             self.acc[at] = self.mine[at] + self.pair[at]
 
+    def spot(self, stage, i, m):
+        r, q4, w = self.r, self.q4, self.w
+        if r.rows_first == (stage == 0):
+            if stage == 1:
+                return (i, slice(None), slice(None), pl.ds(q4, 2 * q4)), self.rows2.at[m]
+            cols = pl.ds(0, w)
+            if r.n2 == 2:
+                cols = pl.ds(pl.multiple_of((1 - r.me2) * q4, q4), 3 * q4)
+            return (i, slice(None), slice(None), cols), self.rows1.at[m, :, :, cols]
+        groups = pl.ds(0, 4) if stage == 0 else pl.ds(1, 2)
+        return (groups, slice(None), slice(None), pl.ds(i * q4, q4)), (self.cols1 if stage == 0 else self.cols2).at[m]
+
     def rim_copy(self, stage, m):
-        r, q4, w = self.r, self.q4, self.w
-        rows = r.rows_first == (stage == 0)
-        k = 1 - m
-        if rows:
-            cols = pl.ds(0, w) if stage == 0 else pl.ds(q4, 2 * q4)
-            src = self.acc.at[3 * k, :, :, cols]
-        else:
-            groups = pl.ds(0, 4) if stage == 0 else pl.ds(1, 2)
-            src = self.acc.at[groups, :, :, pl.ds(3 * k * q4, q4)]
-        rim = self.rims[stage]
-        sides = r.sides1 if stage == 0 else r.sides2
+        sides = self.r.sides1 if stage == 0 else self.r.sides2
+        at, rim = self.spot(stage, 3 * (1 - m), m)
         i = 3 + 2 * stage + m
-        return remote(src, rim.at[m], self.send.at[i], self.recv.at[i], sides[k].where)
+        return remote(self.acc.at[at], rim, self.send.at[i], self.recv.at[i], sides[1 - m].where)
 
     def send_rims(self, stage):
         sides = self.r.sides1 if stage == 0 else self.r.sides2
@@ -242,23 +245,14 @@
             when(sides[1 - m].has)(self.rim_copy(stage, m).start)
 
     def fold(self, stage):
-        r, q4, w, acc = self.r, self.q4, self.w, self.acc
-        rows = r.rows_first == (stage == 0)
-        sides = r.sides1 if stage == 0 else r.sides2
+        sides = self.r.sides1 if stage == 0 else self.r.sides2
         for m in range(2):
 
             @when(sides[m].has)
             def _():
                 self.rim_copy(stage, m).wait_recv()
-                if rows:
-                    cols = pl.ds(0, w) if stage == 0 else pl.ds(q4, 2 * q4)
-                    rim = self.rims[stage]
-                    acc[1 + m, :, :, cols] = acc[1 + m, :, :, cols] + rim[m]
-                else:
-                    groups = pl.ds(0, 4) if stage == 0 else pl.ds(1, 2)
-                    cols = pl.ds((1 + m) * q4, q4)
-                    rim = self.rims[stage]
-                    acc[groups, :, :, cols] = acc[groups, :, :, cols] + rim[m]
+                at, rim = self.spot(stage, 1 + m, m)
+                self.acc[at] = self.acc[at] + rim[...]
 
     def share_copy(self, q):
         return remote(self.core.at[q], self.core.at[q], self.send.at[7], self.recv.at[7], self.partner)
@@ -274,7 +268,7 @@
     def finish(self):
         r = self.r
         for i in range(3):
-            self.needed(i)(self.pair_copy(i).wait_send)
+            self.needed(i, self.other)(self.pair_copy(i, self.other).wait_send)
         for m in range(2):
             when(r.sides1[1 - m].has)(self.rim_copy(0, m).wait_send)
             when(r.sides2[1 - m].has)(self.rim_copy(1, m).wait_send)
@@ -527,8 +521,8 @@
     offsets, spec, *given = refs[:6]
     new_spec, new_probe = refs[6:8]
     pad, probe, amplitudes, table_a, table_b, bufs, grad, prob, total, light_all = refs[8:18]
-    pair, acc, xr, zr, ipair, iacc, ixr, izr, ppair, held, inner, hub, part = refs[18:31]
-    hsend, hrecv, local, gsend, grecv, isend, irecv, psend, precv = refs[31:]
+    pair, acc, xr1, xr2, zr1, zr2, ipair, iacc, ixr, izr, ppair, held, inner, hub, part = refs[18:33]
+    hsend, hrecv, local, gsend, grecv, isend, irecv, psend, precv = refs[33:]
     tile, m = spec.shape[3], probe.shape[1]
     wide = pad.shape[3]
     half = (wide - tile) // 2
@@ -545,15 +539,31 @@
     sides = roles[1].sides1 + roles[0].sides1
     near_greet(ny, partner, roles[1].sides1)
     halos = [Halo(r, spec, pad, hsend, hrecv, partner) for r in roles]
+    folds = [
+        Fold(
+            roles[q],
+            roles[1 - q],
+            grad.at[q],
+            grad.at[1 - q],
+            pair,
+            acc,
+            (zr1, xr1, zr2, xr2),
+            None,
+            gsend,
+            grecv,
+            partner,
+        )
+        for q in range(2)
+    ]
     role = Role(p, nx, ny, 0)
-    fold = Fold(role, grad.at[p], grad.at[1 - p], pair, acc, (xr, zr), None, gsend, grecv, partner)
     light = Fold(
+        role,
         role,
         grad.at[2, :, pl.ds(p, 1)],
         grad.at[2, :, pl.ds(1 - p, 1)],
         ipair,
         iacc,
-        (ixr, izr),
+        (None, ixr, izr, None),
         light_all,
         isend,
         irecv,
@@ -626,11 +636,11 @@
         placer.put(j, 0, pr * dr + pi * di)
         placer.put(j, 1, pr * di - pi * dr)
     gather(1 - p)
-    fold.begin()
+    each(lambda q: folds[q].begin())
     gather(p)
 
     def update(q):
-        q4 = fold.q4
+        q4 = folds[q].q4
         for g in range(2):
             for b in range(2):
                 r0 = (2 * g + b) * h
@@ -642,12 +652,12 @@
 
     def object_last(q):
         light.arrive()
-        fold.fold(1)
+        folds[q].fold(1)
         update(q)
         share_copy(q).start()
 
     def objects(q):
-        probe_sum = probes[q]
+        probe_sum, fold = probes[q], folds[q]
         probe_sum.one()
         fold.add(0)
         fold.add(1)
@@ -657,19 +667,18 @@
         light.share()
         probe_sum.two()
         if q == 0:
-            probe_sum.three(range(chunks // 2))
             fold.fold(0)
             fold.send_rims(1)
-            probe_sum.three(range(chunks // 2, chunks))
+            probe_sum.three()
+            object_last(q)
+            probe_sum.four()
+        else:
+            probe_sum.three()
+            fold.fold(0)
+            fold.send_rims(1)
             probe_sum.four()
             object_last(q)
-        else:
-            probe_sum.three()
-            probe_sum.four()
-            fold.fold(0)
-            fold.send_rims(1)
             probe_sum.five()
-            object_last(q)
 
     each(objects)
 
@@ -679,7 +688,7 @@
         share_copy(1 - q).wait_recv()
         share_copy(q).wait_send()
         light.finish()
-        fold.finish()
+        folds[q].finish()
         probes[q].end()
         halos[q].finish()
 
@@ -726,14 +735,6 @@
     positions = offsets.shape[0]
     held = (probe_wave, amplitudes, consts[0], consts[1])
 
-    def field(size):
-        return [
-            VMEM((4, size, h, wide), f32),
-            VMEM((4, size, h, wide), f32),
-            VMEM((2, 4, size, h, wide // 4), f32),
-            VMEM((2, size, h, wide // 2), f32),
-        ]
-
     step_size = 1.0 / math.sqrt(positions * n * 2)
     results = pl.pallas_call(
         functools.partial(whole_kernel, nx, ny, step_size),
@@ -748,8 +749,16 @@
             VMEM((2, m, m), f32),
             VMEM((2, m, m), f32),
             VMEM((2, 2, 1, h, wide // 2), f32),
-            *field(2),
-            *field(1),
+            VMEM((4, 2, h, wide), f32),
+            VMEM((4, 2, h, wide), f32),
+            VMEM((2, 4, 2, h, wide // 4), f32),
+            VMEM((2, 2, 2, h, wide // 4), f32),
+            VMEM((2, 2, h, wide), f32),
+            VMEM((2, 2, h, wide // 2), f32),
+            VMEM((4, 1, h, wide), f32),
+            VMEM((4, 1, h, wide), f32),
+            VMEM((2, 4, 1, h, wide // 4), f32),
+            VMEM((2, 1, h, wide // 2), f32),
             VMEM((m, m), f32),
             VMEM((ny, m, m), f32),
             VMEM((m, m), f32),

time: 41.2 us -> 39.6 us (0.961)
  Pallas kernels: 40.4 us -> 38.8 us
    pallas_call x1, Pallas kernels: 39.4 us -> 37.8 us  [shards(): pl.pallas_call(functools.partial(whole_kernel, nx, ny, step_size), out_sh...]
where the time goes in v3:
time: 39.6 us; the launch traced here: 39.5 us
  Pallas kernels  38.8 us (98%)
  between operations  0.64 us (2%)
    pallas_call x1, Pallas kernels, shards(): pl.pallas_call(functools.partial(whole_kernel, nx, ny, step_size), out_sh...  37.8 us
    pallas_call x1, Pallas kernels, shards(): pl.pallas_call(emit_kernel, out_shape=[jax.ShapeDtypeStruct(specimen.shap...  1 us

profile of v3, /device:TPU:0, one launch (start us, length us, event | category | flops | bytes accessed | tf_op | source)
XLA Modules:
  0.0 39.5 jit_solution(11818674424174718448)
XLA Ops:
  0.6 37.8 %whole.1 = (f32[2,256,256]{2,1,0:T(8,128)S(1)}, f32[2,256,256]{2,1,0:T(8,128)S(1)}) custom-call(s32[2,2]{1,0:T(2,128)} %refs_0_.1, f32[2,32,8,256]{3,2,1,0:T(8,128)} %bitcast.1, f32[2,256,256]{2,1,0:T(8,128)} %refs_2_.1, bf16[2,256,256]{2,1,0:T(8,128)(2,1)} %refs_3_.1, bf16[512,512]{1,0:T(8,128)(2,1)} %constant.4.clone.refs_4_, ...), custom_call_target="tpu_custom_call" | custom-call | tf_op jit(solution)/shard_map/whole/pallas_call | solution.py:739
  38.5 1.0 %emit.1 = (f32[2,256,256]{2,1,0:T(8,128)}, f32[2,256,256]{2,1,0:T(8,128)}) custom-call(f32[2,256,256]{2,1,0:T(8,128)S(1)} %get-tuple-element.4.spec, f32[2,256,256]{2,1,0:T(8,128)S(1)} %get-tuple-element.5.probe), custom_call_target="tpu_custom_call" | custom-call | tf_op jit(solution)/shard_map/emit/pallas_call | solution.py:780

commit v4 on v3

--- a/solution.py
+++ b/solution.py
@@ -55,7 +55,7 @@
 
 
 def when(*conditions):
-    return pl.when(functools.reduce(jnp.logical_and, conditions))
+    return pl.when(functools.reduce(jnp.logical_and, [c for c in conditions if c is not True]))
 
 
 def dot(a, b):
@@ -66,6 +66,7 @@
     def __init__(self, role, spec, pad, send, recv, partner):
         self.r, self.spec, self.pad, self.partner = role, spec, pad, partner
         self.send, self.recv = send, recv
+        self.direct = not role.rows_first
         tile = spec.shape[3]
         half = (pad.shape[3] - tile) // 2
         self.own = (half, tile)
@@ -98,6 +99,13 @@
         )
 
     def corner(self, m1, m2):
+        if self.direct:
+            return self.copy(
+                self.spec.at[self.at(self.edges[1 - m1], self.edges[1 - m2])],
+                self.pad.at[self.at(self.margins[m1], self.margins[m2])],
+                6 + 2 * m1 + m2,
+                {**self.r.sides1[1 - m1].where, **self.r.sides2[1 - m2].where},
+            )
         return self.copy(
             self.pad.at[self.at(self.margins[m1], self.pad_edges[1 - m2])],
             self.pad.at[self.at(self.margins[m1], self.margins[m2])],
@@ -120,6 +128,10 @@
 
     def begin(self):
         r = self.r
+        if self.direct:
+            for m1 in range(2):
+                for m2 in range(2):
+                    when(r.sides1[1 - m1].has, r.sides2[1 - m2].has)(self.corner(m1, m2).start)
         for m in range(2):
             for e in range(2):
                 when(r.sides1[1 - m].has, r.sides2[e].has)(self.strip1(m, e).start)
@@ -137,7 +149,8 @@
                 @when(r.sides1[m1].has, r.sides2[e].has)
                 def _():
                     self.strip1(m1, e).wait_recv()
-                    self.corner(m1, 1 - e).start()
+                    if not self.direct:
+                        self.corner(m1, 1 - e).start()
                     self.share1(m1, e).start()
 
         for m in range(2):
@@ -185,7 +198,8 @@
             when(r.sides2[m].has)(self.share2(m).wait_send)
         for m1 in range(2):
             for m2 in range(2):
-                when(r.sides1[m1].has, r.sides2[1 - m2].has)(self.corner(m1, m2).wait_send)
+                sent = r.sides1[1 - m1].has if self.direct else r.sides1[m1].has
+                when(sent, r.sides2[1 - m2].has)(self.corner(m1, m2).wait_send)
                 when(r.sides1[m1].has, r.sides2[m2].has)(self.share_corner(m1, m2).wait_send)
 
 
@@ -239,16 +253,16 @@
         i = 3 + 2 * stage + m
         return remote(self.acc.at[at], rim, self.send.at[i], self.recv.at[i], sides[1 - m].where)
 
-    def send_rims(self, stage):
+    def send_rims(self, stage, only=lambda k: True):
         sides = self.r.sides1 if stage == 0 else self.r.sides2
         for m in range(2):
-            when(sides[1 - m].has)(self.rim_copy(stage, m).start)
-
-    def fold(self, stage):
+            when(sides[1 - m].has, only(1 - m))(self.rim_copy(stage, m).start)
+
+    def fold(self, stage, only=lambda k: True):
         sides = self.r.sides1 if stage == 0 else self.r.sides2
         for m in range(2):
 
-            @when(sides[m].has)
+            @when(sides[m].has, only(m))
             def _():
                 self.rim_copy(stage, m).wait_recv()
                 at, rim = self.spot(stage, 1 + m, m)
@@ -285,13 +299,23 @@
         self.chunks = send.shape[1]
         self.rows = prob.shape[1] // self.chunks
         me, mid = lax.axis_index("scanx"), nx // 2
-        step = 2 * (me < mid).astype(jnp.int32) - 1
+        self.lower, self.upper = me < mid, me >= mid
+        step = 2 * self.lower.astype(jnp.int32) - 1
         self.to_inner, self.to_outer = {"scanx": me + step}, {"scanx": me - step}
         self.has_outer = jnp.logical_and(me > 0, me < nx - 1)
         self.no_outer = jnp.logical_not(self.has_outer)
         self.is_hub = jnp.logical_or(me == mid - 1, me == mid)
         self.not_hub = jnp.logical_not(self.is_hub)
         self.mine = lax.axis_index("scany")
+
+    def parts(self):
+        inner = (self.upper, self.lower)
+        return (
+            lambda k: inner[k],
+            lambda k: inner[1 - k],
+            lambda k: jnp.logical_and(inner[k], self.not_hub),
+            lambda k: jnp.logical_or(inner[1 - k], self.is_hub),
+        )
 
     def at(self, c):
         return pl.ds(c * self.rows, self.rows)
@@ -431,12 +455,13 @@
         self.finish(self.held.at[self.mine])
 
 
-def near_greet(ny, partner, sides):
+def near_greet(ny, partner, rows, cols):
     my = lax.axis_index("scany")
     greet(
         [(True, partner)]
         + [(True, {"scany": lax.rem(my + d, ny)}) for d in range(1, ny)]
-        + [(side.has, side.where) for side in sides]
+        + [(side.has, side.where) for side in rows]
+        + [(jnp.logical_and(a.has, b.has), {**a.where, **b.where}) for a in rows for b in cols]
     )
 
 
@@ -537,7 +562,7 @@
         c.start()
     roles = [Role(q, nx, ny) for q in range(2)]
     sides = roles[1].sides1 + roles[0].sides1
-    near_greet(ny, partner, roles[1].sides1)
+    near_greet(ny, partner, roles[1].sides1, roles[0].sides1)
     halos = [Halo(r, spec, pad, hsend, hrecv, partner) for r in roles]
     folds = [
         Fold(
@@ -659,9 +684,13 @@
     def objects(q):
         probe_sum, fold = probes[q], folds[q]
         probe_sum.one()
+        inward, outward, late, early = probe_sum.parts()
         fold.add(0)
         fold.add(1)
-        fold.send_rims(0)
+        if q == 0:
+            fold.send_rims(0)
+        else:
+            fold.send_rims(0, early)
         fold.add(2)
         light.fold(1)
         light.share()
@@ -673,8 +702,10 @@
             object_last(q)
             probe_sum.four()
         else:
+            fold.fold(0, inward)
+            fold.send_rims(0, late)
             probe_sum.three()
-            fold.fold(0)
+            fold.fold(0, outward)
             fold.send_rims(1)
             probe_sum.four()
             object_last(q)
@@ -731,7 +762,7 @@
     dma = pltpu.SemaphoreType.DMA
     n = nx * ny
     h = wide // 8
-    chunks = 4
+    chunks = 8
     positions = offsets.shape[0]
     held = (probe_wave, amplitudes, consts[0], consts[1])
 

time: 39.6 us -> 38.8 us (0.980)
  Pallas kernels: 38.8 us -> 38 us
    pallas_call x1, Pallas kernels: 37.8 us -> 37 us  [shards(): pl.pallas_call(functools.partial(whole_kernel, nx, ny, step_size), out_sh...]
where the time goes in v4:
time: 38.8 us; the launch traced here: 38.6 us
  Pallas kernels  38 us (98%)
  between operations  0.64 us (2%)
    pallas_call x1, Pallas kernels, shards(): pl.pallas_call(functools.partial(whole_kernel, nx, ny, step_size), out_sh...  37 us
    pallas_call x1, Pallas kernels, shards(): pl.pallas_call(emit_kernel, out_shape=[jax.ShapeDtypeStruct(specimen.shap...  1 us

profile of v4, /device:TPU:0, one launch (start us, length us, event | category | flops | bytes accessed | tf_op | source)
XLA Modules:
  0.0 38.6 jit_solution(10100686290316052517)
XLA Ops:
  0.6 37.0 %whole.1 = (f32[2,256,256]{2,1,0:T(8,128)S(1)}, f32[2,256,256]{2,1,0:T(8,128)S(1)}) custom-call(s32[2,2]{1,0:T(2,128)} %refs_0_.1, f32[2,32,8,256]{3,2,1,0:T(8,128)} %bitcast.1, f32[2,256,256]{2,1,0:T(8,128)} %refs_2_.1, bf16[2,256,256]{2,1,0:T(8,128)(2,1)} %refs_3_.1, bf16[512,512]{1,0:T(8,128)(2,1)} %constant.4.clone.refs_4_, ...), custom_call_target="tpu_custom_call" | custom-call | tf_op jit(solution)/shard_map/whole/pallas_call | solution.py:770
  37.6 1.0 %emit.1 = (f32[2,256,256]{2,1,0:T(8,128)}, f32[2,256,256]{2,1,0:T(8,128)}) custom-call(f32[2,256,256]{2,1,0:T(8,128)S(1)} %get-tuple-element.4.spec, f32[2,256,256]{2,1,0:T(8,128)S(1)} %get-tuple-element.5.probe), custom_call_target="tpu_custom_call" | custom-call | tf_op jit(solution)/shard_map/emit/pallas_call | solution.py:811

commit v5 on v4

--- a/solution.py
+++ b/solution.py
@@ -291,13 +291,14 @@
 
 
 class ProbeSum:
-    def __init__(self, q, nx, ny, prob, ppair, held, inner, hub, part, total, send, recv, partner):
+    def __init__(self, q, nx, ny, turn, prob, ppair, held, inner, hub, part, total, send, recv, partner):
         self.q, self.ny = q, ny
         self.prob, self.ppair, self.held = prob, ppair, held
         self.inner, self.hub, self.part, self.total = inner, hub, part, total
         self.send, self.recv, self.partner = send, recv, partner
-        self.chunks = send.shape[1]
-        self.rows = prob.shape[1] // self.chunks
+        chunks = send.shape[1]
+        self.rows = prob.shape[1] // chunks
+        self.list = range(turn * chunks // 2, (turn + 1) * chunks // 2)
         me, mid = lax.axis_index("scanx"), nx // 2
         self.lower, self.upper = me < mid, me >= mid
         step = 2 * self.lower.astype(jnp.int32) - 1
@@ -370,28 +371,31 @@
         when(self.not_hub)(self.inward(c).start)
         when(self.is_hub)(self.across(c).start)
 
-    def collect(self):
+    def collect(self, i):
+        c = self.list[i]
+
         @pl.when(self.has_outer)
         def _():
-            for c in range(self.chunks):
-                self.inward(c).wait_recv()
-                self.part[self.at(c)] = self.part[self.at(c)] + self.inner[self.at(c)]
-                self.send_inward(c)
+            self.inward(c).wait_recv()
+            self.part[self.at(c)] = self.part[self.at(c)] + self.inner[self.at(c)]
+            self.send_inward(c)
 
     def start_part(self, c, value):
         self.part[self.at(c)] = value
         when(self.no_outer)(functools.partial(self.send_inward, c))
 
-    def from_hub(self, hubs, after, chunks=None):
-        @pl.when(self.is_hub if hubs else self.not_hub)
-        def _():
-            for c in chunks or range(self.chunks):
-                self.across(c).wait_recv()
-                value = self.hub[self.at(c)]
-                after(c, self.part[self.at(c)] + value if hubs else value)
+    def from_hub(self, i):
+        c = self.list[i]
+        self.across(c).wait_recv()
+        self.done(c, self.part[self.at(c)] + self.hub[self.at(c)])
+
+    def from_inner(self, i):
+        c = self.list[i]
+        self.across(c).wait_recv()
+        self.done(c, self.hub[self.at(c)])
 
     def finish(self, src):
-        for c in range(self.chunks):
+        for c in self.list:
             self.pair(c).wait_send()
             self.inward(c).wait_send()
             when(self.has_outer)(self.outward(c, src).wait_send)
@@ -402,57 +406,87 @@
 
 class SideFirst(ProbeSum):
     def one(self):
-        for c in range(self.chunks):
+        for c in self.list:
             self.send_sides(c, self.pair_sum(c))
 
-    def two(self):
-        for c in range(self.chunks):
-            self.start_part(c, self.side_sum(c))
-        self.collect()
+    def side(self, i):
+        c = self.list[i]
+        self.start_part(c, self.side_sum(c))
 
     def done(self, c, value):
         self.total[self.q, self.at(c)] = value
         when(self.has_outer)(self.outward(c, self.total.at[self.q]).start)
         self.share(c, self.q).start()
 
-    def three(self, chunks=None):
-        self.from_hub(True, self.done, chunks)
-
-    def four(self):
-        self.from_hub(False, self.done)
-
-    def five(self):
-        pass
-
     def end(self):
         self.finish(self.total.at[self.q])
 
 
 class ChainFirst(ProbeSum):
     def one(self):
-        for c in range(self.chunks):
+        for c in self.list:
             self.start_part(c, self.pair_sum(c))
 
-    def two(self):
-        self.collect()
+    def side(self, i):
+        c = self.list[i]
+        self.total[self.q, self.at(c)] = self.side_sum(c)
+        self.share(c, self.q).start()
 
     def done(self, c, value):
         self.send_sides(c, value)
         when(self.has_outer)(self.outward(c, self.held.at[self.mine]).start)
 
-    def three(self, chunks=None):
-        self.from_hub(True, self.done, chunks)
-
-    def four(self):
-        self.from_hub(False, self.done)
-
-    def five(self):
-        for c in range(self.chunks):
-            self.total[self.q, self.at(c)] = self.side_sum(c)
-            self.share(c, self.q).start()
-
     def end(self):
         self.finish(self.held.at[self.mine])
+
+
+class Both:
+    def __init__(self, q, *args):
+        self.q = q
+        self.a, self.b = SideFirst(q, *args[:2], 0, *args[2:]), ChainFirst(q, *args[:2], 1, *args[2:])
+        self.count = range(len(self.a.list))
+        self.is_hub, self.not_hub, self.parts = self.a.is_hub, self.a.not_hub, self.a.parts
+
+    def one(self):
+        self.b.one()
+        self.a.one()
+
+    def two(self):
+        for i in self.count:
+            self.b.collect(i)
+            self.a.side(i)
+
+    def three(self):
+        for i in self.count:
+            self.a.collect(i)
+
+        @pl.when(self.is_hub)
+        def _():
+            for i in self.count:
+                self.b.from_hub(i)
+
+    def four(self):
+        @pl.when(self.is_hub)
+        def _():
+            for i in self.count:
+                self.a.from_hub(i)
+                self.b.side(i)
+
+        @pl.when(self.not_hub)
+        def _():
+            for i in self.count:
+                self.b.from_inner(i)
+
+    def five(self):
+        @pl.when(self.not_hub)
+        def _():
+            for i in self.count:
+                self.a.from_inner(i)
+                self.b.side(i)
+
+    def end(self):
+        self.a.end()
+        self.b.end()
 
 
 def near_greet(ny, partner, rows, cols):
@@ -594,10 +628,7 @@
         irecv,
         partner,
     )
-    probes = [
-        kind(q, nx, ny, prob, ppair, held, inner, hub, part, total, psend, precv, partner)
-        for q, kind in enumerate((SideFirst, ChainFirst))
-    ]
+    probes = [Both(q, nx, ny, prob, ppair, held, inner, hub, part, total, psend, precv, partner) for q in range(2)]
     placer = Placer(offsets, bufs, m, positions)
 
     def gather(k):
@@ -644,8 +675,6 @@
     pr, pi = probe[0], probe[1]
     windows = [[placer.window(j, pad, k) for k in range(2)] for j in range(positions)]
     fields = [forward(windows[j], pr, pi, table_a, table_b) for j in range(positions)]
-    light.fold(0)
-    light.send_rims(1)
     diffs = [backward(*fields[j], amplitudes[j], table_a, table_b) for j in range(positions)]
     sums = [None, None]
     for (ar, ai), (dr, di) in zip(windows, diffs):
@@ -683,8 +712,8 @@
 
     def objects(q):
         probe_sum, fold = probes[q], folds[q]
+        inward, outward, late, early = probe_sum.parts()
         probe_sum.one()
-        inward, outward, late, early = probe_sum.parts()
         fold.add(0)
         fold.add(1)
         if q == 0:
@@ -692,30 +721,25 @@
         else:
             fold.send_rims(0, early)
         fold.add(2)
+        light.fold(0)
+        light.send_rims(1)
+        probe_sum.two()
+        if q == 1:
+            fold.send_rims(0, late)
+        probe_sum.three()
+        fold.fold(0)
+        fold.send_rims(1)
         light.fold(1)
         light.share()
-        probe_sum.two()
-        if q == 0:
-            fold.fold(0)
-            fold.send_rims(1)
-            probe_sum.three()
-            object_last(q)
-            probe_sum.four()
-        else:
-            fold.fold(0, inward)
-            fold.send_rims(0, late)
-            probe_sum.three()
-            fold.fold(0, outward)
-            fold.send_rims(1)
-            probe_sum.four()
-            object_last(q)
-            probe_sum.five()
+        probe_sum.four()
+        object_last(q)
+        probe_sum.five()
 
     each(objects)
 
     def closing(q):
         for c in range(chunks):
-            probes[q].share(c, 1 - q).wait_recv()
+            probes[q].a.share(c, 1 - q).wait_recv()
         share_copy(1 - q).wait_recv()
         share_copy(q).wait_send()
         light.finish()

time: 38.8 us -> 38.8 us (level)
  no operation moved by 1% of the time
where the time goes in v5:
time: 38.8 us; the launch traced here: 38.7 us
  Pallas kernels  38 us (98%)
  between operations  0.64 us (2%)
    pallas_call x1, Pallas kernels, shards(): pl.pallas_call(functools.partial(whole_kernel, nx, ny, step_size), out_sh...  37 us
    pallas_call x1, Pallas kernels, shards(): pl.pallas_call(emit_kernel, out_shape=[jax.ShapeDtypeStruct(specimen.shap...  1 us

profile of v5, /device:TPU:0, one launch (start us, length us, event | category | flops | bytes accessed | tf_op | source)
XLA Modules:
  0.0 38.7 jit_solution(5999037919038507015)
XLA Ops:
  0.6 37.0 %whole.1 = (f32[2,256,256]{2,1,0:T(8,128)S(1)}, f32[2,256,256]{2,1,0:T(8,128)S(1)}) custom-call(s32[2,2]{1,0:T(2,128)} %refs_0_.1, f32[2,32,8,256]{3,2,1,0:T(8,128)} %bitcast.1, f32[2,256,256]{2,1,0:T(8,128)} %refs_2_.1, bf16[2,256,256]{2,1,0:T(8,128)(2,1)} %refs_3_.1, bf16[512,512]{1,0:T(8,128)(2,1)} %constant.4.clone.refs_4_, ...), custom_call_target="tpu_custom_call" | custom-call | tf_op jit(solution)/shard_map/whole/pallas_call | solution.py:794
  37.7 1.0 %emit.1 = (f32[2,256,256]{2,1,0:T(8,128)}, f32[2,256,256]{2,1,0:T(8,128)}) custom-call(f32[2,256,256]{2,1,0:T(8,128)S(1)} %get-tuple-element.4.spec, f32[2,256,256]{2,1,0:T(8,128)S(1)} %get-tuple-element.5.probe), custom_call_target="tpu_custom_call" | custom-call | tf_op jit(solution)/shard_map/emit/pallas_call | solution.py:835

commit v6 on v4

--- a/solution.py
+++ b/solution.py
@@ -644,8 +644,6 @@
     pr, pi = probe[0], probe[1]
     windows = [[placer.window(j, pad, k) for k in range(2)] for j in range(positions)]
     fields = [forward(windows[j], pr, pi, table_a, table_b) for j in range(positions)]
-    light.fold(0)
-    light.send_rims(1)
     diffs = [backward(*fields[j], amplitudes[j], table_a, table_b) for j in range(positions)]
     sums = [None, None]
     for (ar, ai), (dr, di) in zip(windows, diffs):
@@ -683,30 +681,34 @@
 
     def objects(q):
         probe_sum, fold = probes[q], folds[q]
+        inward, outward, late, early = probe_sum.parts()
         probe_sum.one()
-        inward, outward, late, early = probe_sum.parts()
         fold.add(0)
         fold.add(1)
         if q == 0:
             fold.send_rims(0)
         else:
             fold.send_rims(0, early)
+        light.fold(0)
+        light.send_rims(1)
         fold.add(2)
-        light.fold(1)
-        light.share()
         probe_sum.two()
         if q == 0:
             fold.fold(0)
             fold.send_rims(1)
+            light.fold(1)
+            light.share()
             probe_sum.three()
             object_last(q)
             probe_sum.four()
         else:
+            probe_sum.three()
             fold.fold(0, inward)
             fold.send_rims(0, late)
-            probe_sum.three()
             fold.fold(0, outward)
             fold.send_rims(1)
+            light.fold(1)
+            light.share()
             probe_sum.four()
             object_last(q)
             probe_sum.five()

time: 38.8 us -> 38.5 us (level)
  no operation moved by 1% of the time
where the time goes in v6:
time: 38.5 us; the launch traced here: 38.3 us
  Pallas kernels  37.7 us (98%)
  between operations  0.64 us (2%)
    pallas_call x1, Pallas kernels, shards(): pl.pallas_call(functools.partial(whole_kernel, nx, ny, step_size), out_sh...  36.7 us
    pallas_call x1, Pallas kernels, shards(): pl.pallas_call(emit_kernel, out_shape=[jax.ShapeDtypeStruct(specimen.shap...  1 us

profile of v6, /device:TPU:0, one launch (start us, length us, event | category | flops | bytes accessed | tf_op | source)
XLA Modules:
  0.0 38.3 jit_solution(3853580261691296994)
XLA Ops:
  0.6 36.7 %whole.1 = (f32[2,256,256]{2,1,0:T(8,128)S(1)}, f32[2,256,256]{2,1,0:T(8,128)S(1)}) custom-call(s32[2,2]{1,0:T(2,128)} %refs_0_.1, f32[2,32,8,256]{3,2,1,0:T(8,128)} %bitcast.1, f32[2,256,256]{2,1,0:T(8,128)} %refs_2_.1, bf16[2,256,256]{2,1,0:T(8,128)(2,1)} %refs_3_.1, bf16[512,512]{1,0:T(8,128)(2,1)} %constant.4.clone.refs_4_, ...), custom_call_target="tpu_custom_call" | custom-call | tf_op jit(solution)/shard_map/whole/pallas_call | solution.py:772
  37.3 1.0 %emit.1 = (f32[2,256,256]{2,1,0:T(8,128)}, f32[2,256,256]{2,1,0:T(8,128)}) custom-call(f32[2,256,256]{2,1,0:T(8,128)S(1)} %get-tuple-element.4.spec, f32[2,256,256]{2,1,0:T(8,128)S(1)} %get-tuple-element.5.probe), custom_call_target="tpu_custom_call" | custom-call | tf_op jit(solution)/shard_map/emit/pallas_call | solution.py:813

commit v7 on v4

--- a/solution.py
+++ b/solution.py
@@ -296,7 +296,7 @@
         self.prob, self.ppair, self.held = prob, ppair, held
         self.inner, self.hub, self.part, self.total = inner, hub, part, total
         self.send, self.recv, self.partner = send, recv, partner
-        self.chunks = send.shape[1]
+        self.chunks = recv.shape[1]
         self.rows = prob.shape[1] // self.chunks
         me, mid = lax.axis_index("scanx"), nx // 2
         self.lower, self.upper = me < mid, me >= mid
@@ -314,14 +314,14 @@
             lambda k: inner[k],
             lambda k: inner[1 - k],
             lambda k: jnp.logical_and(inner[k], self.not_hub),
-            lambda k: jnp.logical_or(inner[1 - k], self.is_hub),
+            lambda k: jnp.logical_and(inner[k], self.is_hub),
         )
 
     def at(self, c):
         return pl.ds(c * self.rows, self.rows)
 
     def copy(self, src, dst, s, r, c, where):
-        return remote(src.at[self.at(c)], dst.at[self.at(c)], self.send.at[s, c], self.recv.at[r, c], where)
+        return remote(src.at[self.at(c)], dst.at[self.at(c)], self.send.at[s], self.recv.at[r, c], where)
 
     def pair(self, c):
         return self.copy(self.prob.at[1 - self.q], self.ppair, 0, 0, c, self.partner)
@@ -390,14 +390,15 @@
                 value = self.hub[self.at(c)]
                 after(c, self.part[self.at(c)] + value if hubs else value)
 
-    def finish(self, src):
-        for c in range(self.chunks):
-            self.pair(c).wait_send()
-            self.inward(c).wait_send()
-            when(self.has_outer)(self.outward(c, src).wait_send)
-            self.share(c, self.q).wait_send()
-            for copy in self.sides(c):
-                copy.wait_send()
+    def finish(self):
+        def sent(stage):
+            remote(self.part, self.hub, self.send.at[stage], self.recv.at[2, 0], self.partner).wait_send()
+
+        sent(0)
+        sent(1)
+        pl.when(self.has_outer)(functools.partial(sent, 2))
+        for stage in range(3, 3 + self.ny):
+            sent(stage)
 
 
 class SideFirst(ProbeSum):
@@ -425,7 +426,7 @@
         pass
 
     def end(self):
-        self.finish(self.total.at[self.q])
+        self.finish()
 
 
 class ChainFirst(ProbeSum):
@@ -452,7 +453,7 @@
             self.share(c, self.q).start()
 
     def end(self):
-        self.finish(self.held.at[self.mine])
+        self.finish()
 
 
 def near_greet(ny, partner, rows, cols):
@@ -552,7 +553,7 @@
     wide = pad.shape[3]
     half = (wide - tile) // 2
     h = grad.shape[3]
-    positions, chunks = amplitudes.shape[0], psend.shape[1]
+    positions, chunks = amplitudes.shape[0], precv.shape[1]
     p = lax.axis_index("pos")
     partner = {"pos": 1 - p}
     loads = [pltpu.make_async_copy(spec, pad.at[:, pl.ds(half // 8, tile // 8), :, pl.ds(half, tile)], local.at[0])]
@@ -580,7 +581,7 @@
         )
         for q in range(2)
     ]
-    role = Role(p, nx, ny, 0)
+    role = Role(p, nx, ny, 1)
     light = Fold(
         role,
         role,
@@ -588,7 +589,7 @@
         grad.at[2, :, pl.ds(1 - p, 1)],
         ipair,
         iacc,
-        (None, ixr, izr, None),
+        (izr, None, None, ixr),
         light_all,
         isend,
         irecv,
@@ -634,10 +635,10 @@
         halos[q].relay_corners()
         halos[1 - q].arrive()
 
-    each(strips)
     for i in range(3):
         light.add(i)
     light.send_rims(0)
+    each(strips)
     each(corners)
     for c in loads[:1] + loads[2:]:
         c.wait()
@@ -656,7 +657,7 @@
         at = pl.ds(c * rows, rows)
         for k in range(2):
             prob[k, at] = sums[k][c * rows : (c + 1) * rows]
-        remote(prob.at[1 - p, at], ppair.at[at], psend.at[0, c], precv.at[0, c], partner).start()
+        remote(prob.at[1 - p, at], ppair.at[at], psend.at[0], precv.at[0, c], partner).start()
     for j, (dr, di) in enumerate(diffs):
         placer.put(j, 0, pr * dr + pi * di)
         placer.put(j, 1, pr * di - pi * dr)
@@ -683,14 +684,14 @@
 
     def objects(q):
         probe_sum, fold = probes[q], folds[q]
+        inward, outward, late, middle = probe_sum.parts()
         probe_sum.one()
-        inward, outward, late, early = probe_sum.parts()
         fold.add(0)
         fold.add(1)
         if q == 0:
             fold.send_rims(0)
         else:
-            fold.send_rims(0, early)
+            fold.send_rims(0, outward)
         fold.add(2)
         light.fold(1)
         light.share()
@@ -702,9 +703,10 @@
             object_last(q)
             probe_sum.four()
         else:
+            fold.send_rims(0, middle)
+            probe_sum.three()
             fold.fold(0, inward)
             fold.send_rims(0, late)
-            probe_sum.three()
             fold.fold(0, outward)
             fold.send_rims(1)
             probe_sum.four()
@@ -730,9 +732,10 @@
 
 def emit_kernel(spec, probe, new_spec, new_probe, sem):
     copies = [
-        pltpu.make_async_copy(src.at[k], dst.at[k], sem.at[i, k])
+        pltpu.make_async_copy(src.at[k, at], dst.at[k, at], sem.at[i, k, j])
         for i, (src, dst) in enumerate(((spec, new_spec), (probe, new_probe)))
         for k in range(2)
+        for j, at in enumerate((pl.ds(0, src.shape[1] // 2), pl.ds(src.shape[1] // 2, src.shape[1] // 2)))
     ]
     for c in copies:
         c.start()
@@ -788,8 +791,8 @@
             VMEM((2, 2, h, wide // 2), f32),
             VMEM((4, 1, h, wide), f32),
             VMEM((4, 1, h, wide), f32),
-            VMEM((2, 4, 1, h, wide // 4), f32),
-            VMEM((2, 1, h, wide // 2), f32),
+            VMEM((2, 2, 1, h, wide // 4), f32),
+            VMEM((2, 1, h, wide), f32),
             VMEM((m, m), f32),
             VMEM((ny, m, m), f32),
             VMEM((m, m), f32),
@@ -802,7 +805,7 @@
             dma((8,)),
             dma((8,)),
             dma((8,)),
-            dma((3 + ny, chunks)),
+            dma((3 + ny,)),
             dma((3 + ny, chunks)),
         ],
         compiler_params=pltpu.CompilerParams(vmem_limit_bytes=56 * 2**20, collective_id=0, has_side_effects=True),
@@ -813,7 +816,7 @@
         out_shape=[jax.ShapeDtypeStruct(specimen.shape, f32), jax.ShapeDtypeStruct(probe_wave.shape, f32)],
         in_specs=[vm] * 2,
         out_specs=[pl.BlockSpec(memory_space=pl.ANY)] * 2,
-        scratch_shapes=[dma((2, 2))],
+        scratch_shapes=[dma((2, 2, 2))],
         compiler_params=pltpu.CompilerParams(vmem_limit_bytes=2 * 2**20),
         name="emit",
     )(*results)

time: 38.8 us -> 38.3 us (0.987)
  Pallas kernels: 38 us -> 37.5 us
    pallas_call x1, Pallas kernels: 37 us -> 36.5 us  [shards(): pl.pallas_call(functools.partial(whole_kernel, nx, ny, step_size), out_sh...]
where the time goes in v7:
time: 38.3 us; the launch traced here: 38.2 us
  Pallas kernels  37.5 us (98%)
  between operations  0.64 us (2%)
    pallas_call x1, Pallas kernels, shards(): pl.pallas_call(functools.partial(whole_kernel, nx, ny, step_size), out_sh...  36.5 us
    pallas_call x1, Pallas kernels, shards(): pl.pallas_call(emit_kernel, out_shape=[jax.ShapeDtypeStruct(specimen.shap...  1.03 us

profile of v7, /device:TPU:0, one launch (start us, length us, event | category | flops | bytes accessed | tf_op | source)
XLA Modules:
  0.0 38.2 jit_solution(13483247934025627905)
XLA Ops:
  0.6 36.5 %whole.1 = (f32[2,256,256]{2,1,0:T(8,128)S(1)}, f32[2,256,256]{2,1,0:T(8,128)S(1)}) custom-call(s32[2,2]{1,0:T(2,128)} %refs_0_.1, f32[2,32,8,256]{3,2,1,0:T(8,128)} %bitcast.1, f32[2,256,256]{2,1,0:T(8,128)} %refs_2_.1, bf16[2,256,256]{2,1,0:T(8,128)(2,1)} %refs_3_.1, bf16[512,512]{1,0:T(8,128)(2,1)} %constant.4.clone.refs_4_, ...), custom_call_target="tpu_custom_call" | custom-call | tf_op jit(solution)/shard_map/whole/pallas_call | solution.py:773
  37.1 1.0 %emit.1 = (f32[2,256,256]{2,1,0:T(8,128)}, f32[2,256,256]{2,1,0:T(8,128)}) custom-call(f32[2,256,256]{2,1,0:T(8,128)S(1)} %get-tuple-element.4.spec, f32[2,256,256]{2,1,0:T(8,128)S(1)} %get-tuple-element.5.probe), custom_call_target="tpu_custom_call" | custom-call | tf_op jit(solution)/shard_map/emit/pallas_call | solution.py:814

commit v8 on v7

--- a/solution.py
+++ b/solution.py
@@ -128,10 +128,6 @@
 
     def begin(self):
         r = self.r
-        if self.direct:
-            for m1 in range(2):
-                for m2 in range(2):
-                    when(r.sides1[1 - m1].has, r.sides2[1 - m2].has)(self.corner(m1, m2).start)
         for m in range(2):
             for e in range(2):
                 when(r.sides1[1 - m].has, r.sides2[e].has)(self.strip1(m, e).start)
@@ -141,6 +137,12 @@
             for e in range(2):
                 when(r.sides1[1 - m].has, jnp.logical_not(r.sides2[e].has))(self.strip1(m, e).start)
 
+    def begin_corners(self):
+        r = self.r
+        for m1 in range(2):
+            for m2 in range(2):
+                when(r.sides1[1 - m1].has, r.sides2[1 - m2].has)(self.corner(m1, m2).start)
+
     def relay(self):
         r = self.r
         for m1 in range(2):
@@ -153,20 +155,22 @@
                         self.corner(m1, 1 - e).start()
                     self.share1(m1, e).start()
 
+        for m1 in range(2):
+            for e in range(2):
+
+                @when(r.sides1[m1].has, jnp.logical_not(r.sides2[e].has))
+                def _():
+                    self.strip1(m1, e).wait_recv()
+                    self.share1(m1, e).start()
+
+    def relay_second(self):
+        r = self.r
         for m in range(2):
 
             @when(r.sides2[m].has)
             def _():
                 self.strip2(m).wait_recv()
                 self.share2(m).start()
-
-        for m1 in range(2):
-            for e in range(2):
-
-                @when(r.sides1[m1].has, jnp.logical_not(r.sides2[e].has))
-                def _():
-                    self.strip1(m1, e).wait_recv()
-                    self.share1(m1, e).start()
 
     def relay_corners(self):
         r = self.r
@@ -214,8 +218,14 @@
     def piece(self, i, r):
         q4, cols = self.q4, (slice(None),) * 3
         if r.rows_first:
-            return ((pl.ds(0, 1),), (pl.ds(3, 1),), (pl.ds(1, 2),))[i]
+            return ((pl.ds(0, 1), pl.ds(3, 1), pl.ds(1, 2))[i], slice(None), slice(None), self.columns())
         return cols + ((pl.ds(0, q4),), (pl.ds(3 * q4, q4),), (pl.ds(q4, 2 * q4),))[i]
+
+    def columns(self):
+        q4 = self.q4
+        if self.r.n2 == 2 and self.r.rows_first:
+            return pl.ds(pl.multiple_of((1 - self.r.me2) * q4, q4), 3 * q4)
+        return pl.ds(0, self.w)
 
     def needed(self, i, r):
         return pl.when(r.sides1[i].has) if i < 2 else lambda f: f()
@@ -240,9 +250,7 @@
         if r.rows_first == (stage == 0):
             if stage == 1:
                 return (i, slice(None), slice(None), pl.ds(q4, 2 * q4)), self.rows2.at[m]
-            cols = pl.ds(0, w)
-            if r.n2 == 2:
-                cols = pl.ds(pl.multiple_of((1 - r.me2) * q4, q4), 3 * q4)
+            cols = self.columns()
             return (i, slice(None), slice(None), cols), self.rows1.at[m, :, :, cols]
         groups = pl.ds(0, 4) if stage == 0 else pl.ds(1, 2)
         return (groups, slice(None), slice(None), pl.ds(i * q4, q4)), (self.cols1 if stage == 0 else self.cols2).at[m]
@@ -291,179 +299,170 @@
 
 
 class ProbeSum:
-    def __init__(self, q, nx, ny, prob, ppair, held, inner, hub, part, total, send, recv, partner):
-        self.q, self.ny = q, ny
-        self.prob, self.ppair, self.held = prob, ppair, held
-        self.inner, self.hub, self.part, self.total = inner, hub, part, total
+    PAIR, INNER, OUTER, ROW = range(4)
+
+    def __init__(self, q, nx, ny, prob, ppair, row_in, out_in, part, hub, total, send, recv, shared, partner):
+        self.q, self.ny, self.chunks = q, ny, range(recv.shape[1])
+        self.shared_sems = shared
+        self.prob, self.ppair, self.row_in, self.out_in = prob, ppair, row_in, out_in
+        self.part, self.hub, self.total = part, hub, total
         self.send, self.recv, self.partner = send, recv, partner
-        self.chunks = recv.shape[1]
-        self.rows = prob.shape[1] // self.chunks
+        self.size = prob.shape[1] // ny
+        self.rows = self.size // len(self.chunks)
         me, mid = lax.axis_index("scanx"), nx // 2
         self.lower, self.upper = me < mid, me >= mid
         step = 2 * self.lower.astype(jnp.int32) - 1
-        self.to_inner, self.to_outer = {"scanx": me + step}, {"scanx": me - step}
+        self.inner, self.outer = {"scanx": me + step}, {"scanx": me - step}
         self.has_outer = jnp.logical_and(me > 0, me < nx - 1)
-        self.no_outer = jnp.logical_not(self.has_outer)
         self.is_hub = jnp.logical_or(me == mid - 1, me == mid)
         self.not_hub = jnp.logical_not(self.is_hub)
         self.mine = lax.axis_index("scany")
 
-    def parts(self):
-        inner = (self.upper, self.lower)
-        return (
-            lambda k: inner[k],
-            lambda k: inner[1 - k],
-            lambda k: jnp.logical_and(inner[k], self.not_hub),
-            lambda k: jnp.logical_and(inner[k], self.is_hub),
-        )
-
-    def at(self, c):
-        return pl.ds(c * self.rows, self.rows)
+    def column(self, d):
+        return lax.rem(self.mine + d, self.ny)
+
+    def origin(self, d):
+        return lax.rem(self.mine - d + self.ny, self.ny)
+
+    def at(self, h, c):
+        if isinstance(h, int):
+            return pl.ds(h * self.size + c * self.rows, self.rows)
+        return pl.ds(pl.multiple_of(h * self.size + c * self.rows, 8), self.rows)
 
     def copy(self, src, dst, s, r, c, where):
-        return remote(src.at[self.at(c)], dst.at[self.at(c)], self.send.at[s], self.recv.at[r, c], where)
-
-    def pair(self, c):
-        return self.copy(self.prob.at[1 - self.q], self.ppair, 0, 0, c, self.partner)
-
-    def inward(self, c):
-        return self.copy(self.part, self.inner, 1, 1, c, self.to_inner)
-
-    def across(self, c):
-        return self.copy(self.part, self.hub, 1, 2, c, self.to_inner)
-
-    def outward(self, c, src):
-        return self.copy(src, self.hub, 2, 2, c, self.to_outer)
-
-    def share(self, c, q):
-        return self.copy(self.total.at[q], self.total.at[q], 3, 3, c, self.partner)
-
-    def sides(self, c):
-        out = []
+        return remote(src, dst, self.send.at[s], self.recv.at[r, c], where)
+
+    def pair(self, h, c):
+        at = self.at(h, c)
+        return self.copy(self.prob.at[1 - self.q, at], self.ppair.at[at], self.PAIR, self.PAIR, c, self.partner)
+
+    def to_owner(self, d, c):
+        to = self.column(d)
+        src, dst = self.ppair.at[self.at(to, c)], self.row_in.at[self.mine, self.at(0, c)]
+        return self.copy(src, dst, self.ROW + d - 1, self.ROW + d - 1, c, {"scany": to})
+
+    def pass_in(self, c):
+        at = self.at(0, c)
+        return self.copy(self.part.at[at], self.out_in.at[at], self.INNER, self.INNER, c, self.inner)
+
+    def between_hubs(self, c):
+        at = self.at(0, c)
+        return self.copy(self.part.at[at], self.hub.at[at], self.INNER, self.OUTER, c, self.inner)
+
+    def pass_out(self, c):
+        src, dst = self.total.at[self.q, self.at(self.mine, c)], self.hub.at[self.at(0, c)]
+        return self.copy(src, dst, self.OUTER, self.OUTER, c, self.outer)
+
+    def to_row(self, d, c):
+        ref = self.total.at[self.q, self.at(self.mine, c)]
+        return self.copy(ref, ref, self.ROW + self.ny + d - 2, self.ROW + self.ny + d - 2, c, {"scany": self.column(d)})
+
+    def share(self, d, c, q):
+        ref = self.total.at[q, self.at(self.origin(d), c)]
+        return remote(ref, ref, self.shared_sems.at[0], self.shared_sems.at[1], self.partner)
+
+    def wait(self, ref, r, c):
+        self.copy(ref, ref, self.PAIR, r, c, self.partner).wait_recv()
+
+    def one(self):
+        for c in self.chunks:
+            self.wait(self.ppair.at[pl.ds(0, self.ny * self.rows)], self.PAIR, c)
+            for h in range(self.ny):
+                at = self.at(h, c)
+                self.ppair[at] = self.prob[self.q, at] + self.ppair[at]
+            for d in range(1, self.ny):
+                self.to_owner(d, c).start()
+
+    def two(self):
+        for c in self.chunks:
+            at = self.at(0, c)
+            value = self.ppair[self.at(self.mine, c)]
+            for d in range(1, self.ny):
+                slot = self.row_in.at[self.origin(d), at]
+                self.wait(slot, self.ROW + d - 1, c)
+                value = value + slot[...]
+            self.part[at] = value
+
+            @pl.when(self.has_outer)
+            def _():
+                slot = self.out_in.at[at]
+                self.wait(slot, self.INNER, c)
+                self.part[at] = self.part[at] + slot[...]
+
+            pl.when(self.is_hub)(self.between_hubs(c).start)
+            pl.when(self.not_hub)(self.pass_in(c).start)
+
+    def inward(self, k):
+        return self.upper if k == 0 else self.lower
+
+    def late(self, k):
+        return jnp.logical_and(self.inward(k), self.not_hub)
+
+    def early(self, k):
+        return jnp.logical_not(self.late(k))
+
+    def three(self, chunks):
+        for c in chunks:
+            at, mine = self.at(0, c), self.at(self.mine, c)
+            self.wait(self.hub.at[at], self.OUTER, c)
+
+            @pl.when(self.is_hub)
+            def _():
+                self.total[self.q, mine] = self.part[at] + self.hub[at]
+
+            @pl.when(self.not_hub)
+            def _():
+                self.total[self.q, mine] = self.hub[at]
+
+            pl.when(self.has_outer)(self.pass_out(c).start)
+            for d in range(1, self.ny):
+                self.to_row(d, c).start()
+            self.share(0, c, self.q).start()
+
+    def four(self):
+        for c in self.chunks:
+            for d in range(1, self.ny):
+                self.wait(self.total.at[self.q, self.at(self.origin(d), c)], self.ROW + self.ny + d - 2, c)
+                self.share(d, c, self.q).start()
+
+    def shared(self):
+        ref = self.total.at[1 - self.q]
+        remote(ref, ref, self.shared_sems.at[0], self.shared_sems.at[1], self.partner).wait_recv()
+
+    def end(self):
+        def sent(ref, stage):
+            remote(ref, ref, self.send.at[stage], self.recv.at[0, 0], self.partner).wait_send()
+
+        sent(self.ppair, self.PAIR)
+        ref = self.total.at[self.q]
+        remote(ref, ref, self.shared_sems.at[0], self.shared_sems.at[1], self.partner).wait_send()
+        sent(self.part, self.INNER)
+        pl.when(self.has_outer)(functools.partial(sent, self.part, self.OUTER))
         for d in range(1, self.ny):
-            slot = self.held.at[self.mine]
-            out.append(self.copy(slot, slot, 3 + d, 3 + d, c, {"scany": lax.rem(self.mine + d, self.ny)}))
-        return out
-
-    def side_arrive(self, c):
-        for d in range(1, self.ny):
-            slot = self.held.at[lax.rem(self.mine - d + self.ny, self.ny)]
-            self.copy(slot, slot, 3 + d, 3 + d, c, self.partner).wait_recv()
-
-    def side_sum(self, c):
-        self.side_arrive(c)
-        out = self.held[0, self.at(c)]
-        for i in range(1, self.ny):
-            out = out + self.held[i, self.at(c)]
-        return out
-
-    def pair_sum(self, c):
-        self.pair(c).wait_recv()
-        return self.prob[self.q, self.at(c)] + self.ppair[self.at(c)]
-
-    def send_sides(self, c, value):
-        self.held[self.mine, self.at(c)] = value
-        for copy in self.sides(c):
-            copy.start()
-
-    def send_inward(self, c):
-        when(self.not_hub)(self.inward(c).start)
-        when(self.is_hub)(self.across(c).start)
-
-    def collect(self):
-        @pl.when(self.has_outer)
-        def _():
-            for c in range(self.chunks):
-                self.inward(c).wait_recv()
-                self.part[self.at(c)] = self.part[self.at(c)] + self.inner[self.at(c)]
-                self.send_inward(c)
-
-    def start_part(self, c, value):
-        self.part[self.at(c)] = value
-        when(self.no_outer)(functools.partial(self.send_inward, c))
-
-    def from_hub(self, hubs, after, chunks=None):
-        @pl.when(self.is_hub if hubs else self.not_hub)
-        def _():
-            for c in chunks or range(self.chunks):
-                self.across(c).wait_recv()
-                value = self.hub[self.at(c)]
-                after(c, self.part[self.at(c)] + value if hubs else value)
-
-    def finish(self):
-        def sent(stage):
-            remote(self.part, self.hub, self.send.at[stage], self.recv.at[2, 0], self.partner).wait_send()
-
-        sent(0)
-        sent(1)
-        pl.when(self.has_outer)(functools.partial(sent, 2))
-        for stage in range(3, 3 + self.ny):
-            sent(stage)
-
-
-class SideFirst(ProbeSum):
-    def one(self):
-        for c in range(self.chunks):
-            self.send_sides(c, self.pair_sum(c))
-
-    def two(self):
-        for c in range(self.chunks):
-            self.start_part(c, self.side_sum(c))
-        self.collect()
-
-    def done(self, c, value):
-        self.total[self.q, self.at(c)] = value
-        when(self.has_outer)(self.outward(c, self.total.at[self.q]).start)
-        self.share(c, self.q).start()
-
-    def three(self, chunks=None):
-        self.from_hub(True, self.done, chunks)
-
-    def four(self):
-        self.from_hub(False, self.done)
-
-    def five(self):
-        pass
-
-    def end(self):
-        self.finish()
-
-
-class ChainFirst(ProbeSum):
-    def one(self):
-        for c in range(self.chunks):
-            self.start_part(c, self.pair_sum(c))
-
-    def two(self):
-        self.collect()
-
-    def done(self, c, value):
-        self.send_sides(c, value)
-        when(self.has_outer)(self.outward(c, self.held.at[self.mine]).start)
-
-    def three(self, chunks=None):
-        self.from_hub(True, self.done, chunks)
-
-    def four(self):
-        self.from_hub(False, self.done)
-
-    def five(self):
-        for c in range(self.chunks):
-            self.total[self.q, self.at(c)] = self.side_sum(c)
-            self.share(c, self.q).start()
-
-    def end(self):
-        self.finish()
-
-
-def near_greet(ny, partner, rows, cols):
+            sent(self.part, self.ROW + d - 1)
+            sent(self.part, self.ROW + self.ny + d - 2)
+
+
+def near_greet(ny, partner, rows):
     my = lax.axis_index("scany")
     greet(
         [(True, partner)]
         + [(True, {"scany": lax.rem(my + d, ny)}) for d in range(1, ny)]
         + [(side.has, side.where) for side in rows]
-        + [(jnp.logical_and(a.has, b.has), {**a.where, **b.where}) for a in rows for b in cols]
     )
+
+
+def row_ready(sem, rows):
+    for i, side in enumerate(rows):
+
+        @pl.when(side.has)
+        def _(i=i, side=side):
+            pl.semaphore_signal(sem.at[1 - i], inc=1, device_id=side.where, device_id_type=MESH)
+
+
+def row_wait(sem, rows):
+    for i, side in enumerate(rows):
+        pl.when(side.has)(functools.partial(pl.semaphore_wait, sem.at[i], 1))
 
 
 def each(step):
@@ -547,8 +546,8 @@
     offsets, spec, *given = refs[:6]
     new_spec, new_probe = refs[6:8]
     pad, probe, amplitudes, table_a, table_b, bufs, grad, prob, total, light_all = refs[8:18]
-    pair, acc, xr1, xr2, zr1, zr2, ipair, iacc, ixr, izr, ppair, held, inner, hub, part = refs[18:33]
-    hsend, hrecv, local, gsend, grecv, isend, irecv, psend, precv = refs[33:]
+    pair, acc, xr2, zr1, ipair, iacc, ixr, izr, ppair, row_in, out_in, part, hub = refs[18:31]
+    hsend, hrecv, local, gsend, grecv, isend, irecv, psend, precv, ssems, ready = refs[31:]
     tile, m = spec.shape[3], probe.shape[1]
     wide = pad.shape[3]
     half = (wide - tile) // 2
@@ -563,25 +562,10 @@
         c.start()
     roles = [Role(q, nx, ny) for q in range(2)]
     sides = roles[1].sides1 + roles[0].sides1
-    near_greet(ny, partner, roles[1].sides1, roles[0].sides1)
+    near_greet(ny, partner, roles[1].sides1)
     halos = [Halo(r, spec, pad, hsend, hrecv, partner) for r in roles]
-    folds = [
-        Fold(
-            roles[q],
-            roles[1 - q],
-            grad.at[q],
-            grad.at[1 - q],
-            pair,
-            acc,
-            (zr1, xr1, zr2, xr2),
-            None,
-            gsend,
-            grecv,
-            partner,
-        )
-        for q in range(2)
-    ]
     role = Role(p, nx, ny, 1)
+    fold = Fold(role, role, grad.at[p], grad.at[1 - p], pair, acc, (zr1, None, None, xr2), None, gsend, grecv, partner)
     light = Fold(
         role,
         role,
@@ -595,10 +579,7 @@
         irecv,
         partner,
     )
-    probes = [
-        kind(q, nx, ny, prob, ppair, held, inner, hub, part, total, psend, precv, partner)
-        for q, kind in enumerate((SideFirst, ChainFirst))
-    ]
+    probe_sum = ProbeSum(p, nx, ny, prob, ppair, row_in, out_in, part, hub, total, psend, precv, ssems, partner)
     placer = Placer(offsets, bufs, m, positions)
 
     def gather(k):
@@ -606,6 +587,8 @@
             for b in range(2):
                 grad[k, g, b] = placer.rows(k, (2 * g + b) * h, h)
 
+    rows = roles[1].sides1
+    pl.when(p == 0)(functools.partial(row_ready, ready, rows))
     each(lambda q: halos[q].begin())
     for i, at in enumerate(
         (
@@ -621,6 +604,12 @@
             pad[at] = jnp.zeros(pad.at[at].shape, pad.dtype)
 
     placer.clear()
+
+    @pl.when(p == 0)
+    def _():
+        row_wait(ready, rows)
+        halos[0].begin_corners()
+
     loads[1].wait()
     power = probe[0] * probe[0] + probe[1] * probe[1]
     for j in range(positions):
@@ -632,6 +621,7 @@
         halos[q].relay()
 
     def corners(q):
+        halos[q].relay_second()
         halos[q].relay_corners()
         halos[1 - q].arrive()
 
@@ -652,80 +642,56 @@
     for (ar, ai), (dr, di) in zip(windows, diffs):
         for k, t in enumerate((ar * dr + ai * di, ar * di - ai * dr)):
             sums[k] = t if sums[k] is None else sums[k] + t
-    rows = m // chunks
     for c in range(chunks):
-        at = pl.ds(c * rows, rows)
-        for k in range(2):
-            prob[k, at] = sums[k][c * rows : (c + 1) * rows]
-        remote(prob.at[1 - p, at], ppair.at[at], psend.at[0], precv.at[0, c], partner).start()
+        for part_of in range(ny):
+            at = probe_sum.at(part_of, c)
+            for k in range(2):
+                prob[k, at] = sums[k][at.start : at.start + at.size]
+            probe_sum.pair(part_of, c).start()
     for j, (dr, di) in enumerate(diffs):
         placer.put(j, 0, pr * dr + pi * di)
         placer.put(j, 1, pr * di - pi * dr)
     gather(1 - p)
-    each(lambda q: folds[q].begin())
+    fold.begin()
     gather(p)
-
-    def update(q):
-        q4 = folds[q].q4
-        for g in range(2):
-            for b in range(2):
-                r0 = (2 * g + b) * h
-                old = pad[q, (half + r0) // 8 : (half + r0 + h) // 8, :, half : half + tile].reshape(h, tile)
-                new_spec[q, r0 : r0 + h] = old + acc[1 + g, b, :, q4 : 3 * q4] / (light_all[b, g, 0] + 1.0)
 
     def share_copy(q):
         return remote(new_spec.at[q], new_spec.at[q], gsend.at[7], grecv.at[7], partner)
 
-    def object_last(q):
-        light.arrive()
-        folds[q].fold(1)
-        update(q)
-        share_copy(q).start()
-
-    def objects(q):
-        probe_sum, fold = probes[q], folds[q]
-        inward, outward, late, middle = probe_sum.parts()
-        probe_sum.one()
-        fold.add(0)
-        fold.add(1)
-        if q == 0:
-            fold.send_rims(0)
-        else:
-            fold.send_rims(0, outward)
-        fold.add(2)
-        light.fold(1)
-        light.share()
-        probe_sum.two()
-        if q == 0:
-            fold.fold(0)
-            fold.send_rims(1)
-            probe_sum.three()
-            object_last(q)
-            probe_sum.four()
-        else:
-            fold.send_rims(0, middle)
-            probe_sum.three()
-            fold.fold(0, inward)
-            fold.send_rims(0, late)
-            fold.fold(0, outward)
-            fold.send_rims(1)
-            probe_sum.four()
-            object_last(q)
-            probe_sum.five()
-
-    each(objects)
-
-    def closing(q):
-        for c in range(chunks):
-            probes[q].share(c, 1 - q).wait_recv()
-        share_copy(1 - q).wait_recv()
-        share_copy(q).wait_send()
-        light.finish()
-        folds[q].finish()
-        probes[q].end()
-        halos[q].finish()
-
-    each(closing)
+    probe_sum.one()
+    fold.add(0)
+    fold.add(1)
+    fold.send_rims(0, probe_sum.early)
+    fold.add(2)
+    light.fold(1)
+    light.share()
+    probe_sum.two()
+    fold.send_rims(0, probe_sum.late)
+
+    def strips_in():
+        fold.fold(0)
+        fold.send_rims(1)
+
+    pl.when(jnp.logical_not(probe_sum.has_outer))(strips_in)
+    probe_sum.three(range(chunks))
+    pl.when(probe_sum.has_outer)(strips_in)
+    light.arrive()
+    fold.fold(1)
+    q4 = fold.q4
+    for g in range(2):
+        for b in range(2):
+            r0 = (2 * g + b) * h
+            old = pad[p, (half + r0) // 8 : (half + r0 + h) // 8, :, half : half + tile].reshape(h, tile)
+            new_spec[p, r0 : r0 + h] = old + acc[1 + g, b, :, q4 : 3 * q4] / (light_all[b, g, 0] + 1.0)
+    share_copy(p).start()
+    probe_sum.four()
+    probe_sum.shared()
+    share_copy(1 - p).wait_recv()
+    share_copy(p).wait_send()
+    light.finish()
+    fold.finish()
+    probe_sum.end()
+    each(lambda q: halos[q].finish())
     for k in range(2):
         new_probe[k] = probe[k] + total[k] * step_size
 
@@ -785,19 +751,17 @@
             VMEM((2, 2, 1, h, wide // 2), f32),
             VMEM((4, 2, h, wide), f32),
             VMEM((4, 2, h, wide), f32),
-            VMEM((2, 4, 2, h, wide // 4), f32),
             VMEM((2, 2, 2, h, wide // 4), f32),
             VMEM((2, 2, h, wide), f32),
-            VMEM((2, 2, h, wide // 2), f32),
             VMEM((4, 1, h, wide), f32),
             VMEM((4, 1, h, wide), f32),
             VMEM((2, 2, 1, h, wide // 4), f32),
             VMEM((2, 1, h, wide), f32),
             VMEM((m, m), f32),
-            VMEM((ny, m, m), f32),
-            VMEM((m, m), f32),
-            VMEM((m, m), f32),
-            VMEM((m, m), f32),
+            VMEM((ny, m // ny, m), f32),
+            VMEM((m // ny, m), f32),
+            VMEM((m // ny, m), f32),
+            VMEM((m // ny, m), f32),
             dma((20,)),
             dma((20,)),
             dma((5,)),
@@ -805,8 +769,10 @@
             dma((8,)),
             dma((8,)),
             dma((8,)),
-            dma((3 + ny,)),
-            dma((3 + ny, chunks)),
+            dma((1 + 2 * ny,)),
+            dma((1 + 2 * ny, chunks)),
+            dma((2,)),
+            pltpu.SemaphoreType.REGULAR((2,)),
         ],
         compiler_params=pltpu.CompilerParams(vmem_limit_bytes=56 * 2**20, collective_id=0, has_side_effects=True),
         name="whole",

time: 38.3 us -> 37.1 us (0.969)
  Pallas kernels: 37.5 us -> 36.3 us
    pallas_call x1, Pallas kernels: 36.5 us -> 35.3 us  [shards(): pl.pallas_call(functools.partial(whole_kernel, nx, ny, step_size), out_sh...]
where the time goes in v8:
time: 37.1 us; the launch traced here: 36.9 us
  Pallas kernels  36.3 us (98%)
  between operations  0.64 us (2%)
    pallas_call x1, Pallas kernels, shards(): pl.pallas_call(functools.partial(whole_kernel, nx, ny, step_size), out_sh...  35.3 us
    pallas_call x1, Pallas kernels, shards(): pl.pallas_call(emit_kernel, out_shape=[jax.ShapeDtypeStruct(specimen.shap...  1.03 us

profile of v8, /device:TPU:0, one launch (start us, length us, event | category | flops | bytes accessed | tf_op | source)
XLA Modules:
  0.0 36.9 jit_solution(13277199156491319535)
XLA Ops:
  0.6 35.3 %whole.1 = (f32[2,256,256]{2,1,0:T(8,128)S(1)}, f32[2,256,256]{2,1,0:T(8,128)S(1)}) custom-call(s32[2,2]{1,0:T(2,128)} %refs_0_.1, f32[2,32,8,256]{3,2,1,0:T(8,128)} %bitcast.1, f32[2,256,256]{2,1,0:T(8,128)} %refs_2_.1, bf16[2,256,256]{2,1,0:T(8,128)(2,1)} %refs_3_.1, bf16[512,512]{1,0:T(8,128)(2,1)} %constant.4.clone.refs_4_, ...), custom_call_target="tpu_custom_call" | custom-call | tf_op jit(solution)/shard_map/whole/pallas_call | solution.py:739
  35.9 1.0 %emit.1 = (f32[2,256,256]{2,1,0:T(8,128)}, f32[2,256,256]{2,1,0:T(8,128)}) custom-call(f32[2,256,256]{2,1,0:T(8,128)S(1)} %get-tuple-element.4.spec, f32[2,256,256]{2,1,0:T(8,128)S(1)} %get-tuple-element.5.probe), custom_call_target="tpu_custom_call" | custom-call | tf_op jit(solution)/shard_map/emit/pallas_call | solution.py:780

commit v9 on v8

--- a/solution.py
+++ b/solution.py
@@ -316,6 +316,11 @@
         self.has_outer = jnp.logical_and(me > 0, me < nx - 1)
         self.is_hub = jnp.logical_or(me == mid - 1, me == mid)
         self.not_hub = jnp.logical_not(self.is_hub)
+        self.is_last = jnp.logical_and(self.not_hub, jnp.logical_not(self.has_outer))
+        self.not_last = jnp.logical_not(self.is_last)
+        near_end = jnp.logical_or(me == 1, me == nx - 2)
+        self.outer_last = jnp.logical_and(self.has_outer, near_end)
+        self.first_direct = len(self.chunks) - len(self.chunks) * 4 // 8
         self.mine = lax.axis_index("scany")
 
     def column(self, d):
@@ -356,6 +361,11 @@
     def to_row(self, d, c):
         ref = self.total.at[self.q, self.at(self.mine, c)]
         return self.copy(ref, ref, self.ROW + self.ny + d - 2, self.ROW + self.ny + d - 2, c, {"scany": self.column(d)})
+
+    def to_end(self, d, c):
+        ref = self.total.at[self.q, self.at(self.mine, c)]
+        where = {"scanx": self.outer["scanx"], "scany": self.column(d)}
+        return remote(ref, ref, self.shared_sems.at[1 + d], self.recv.at[self.ROW + self.ny + d - 2, c], where)
 
     def share(self, d, c, q):
         ref = self.total.at[q, self.at(self.origin(d), c)]
@@ -416,7 +426,11 @@
 
             pl.when(self.has_outer)(self.pass_out(c).start)
             for d in range(1, self.ny):
-                self.to_row(d, c).start()
+                if c < self.first_direct:
+                    self.to_row(d, c).start()
+                else:
+                    pl.when(self.outer_last)(self.to_end(d, c).start)
+                    pl.when(self.not_last)(self.to_row(d, c).start)
             self.share(0, c, self.q).start()
 
     def four(self):
@@ -440,7 +454,15 @@
         pl.when(self.has_outer)(functools.partial(sent, self.part, self.OUTER))
         for d in range(1, self.ny):
             sent(self.part, self.ROW + d - 1)
-            sent(self.part, self.ROW + self.ny + d - 2)
+            first = self.first_direct * self.rows
+            stage = self.ROW + self.ny + d - 2
+            pl.when(self.not_last)(functools.partial(sent, self.part, stage))
+            pl.when(self.is_last)(functools.partial(sent, self.part.at[pl.ds(0, first)], stage))
+
+            @pl.when(self.outer_last)
+            def _():
+                ref = self.part.at[pl.ds(0, self.size - first)]
+                remote(ref, ref, self.shared_sems.at[1 + d], self.recv.at[0, 0], self.partner).wait_send()
 
 
 def near_greet(ny, partner, rows):
@@ -771,7 +793,7 @@
             dma((8,)),
             dma((1 + 2 * ny,)),
             dma((1 + 2 * ny, chunks)),
-            dma((2,)),
+            dma((1 + ny,)),
             pltpu.SemaphoreType.REGULAR((2,)),
         ],
         compiler_params=pltpu.CompilerParams(vmem_limit_bytes=56 * 2**20, collective_id=0, has_side_effects=True),

time: 37.1 us -> 36.3 us (0.978)
  Pallas kernels: 36.3 us -> 35.5 us
    pallas_call x1, Pallas kernels: 35.3 us -> 34.5 us  [shards(): pl.pallas_call(functools.partial(whole_kernel, nx, ny, step_size), out_sh...]
where the time goes in v9:
time: 36.3 us; the launch traced here: 36.2 us
  Pallas kernels  35.5 us (98%)
  between operations  0.64 us (2%)
    pallas_call x1, Pallas kernels, shards(): pl.pallas_call(functools.partial(whole_kernel, nx, ny, step_size), out_sh...  34.5 us
    pallas_call x1, Pallas kernels, shards(): pl.pallas_call(emit_kernel, out_shape=[jax.ShapeDtypeStruct(specimen.shap...  1.03 us

profile of v9, /device:TPU:0, one launch (start us, length us, event | category | flops | bytes accessed | tf_op | source)
XLA Modules:
  0.0 36.2 jit_solution(2419217199333287772)
XLA Ops:
  0.6 34.5 %whole.1 = (f32[2,256,256]{2,1,0:T(8,128)S(1)}, f32[2,256,256]{2,1,0:T(8,128)S(1)}) custom-call(s32[2,2]{1,0:T(2,128)} %refs_0_.1, f32[2,32,8,256]{3,2,1,0:T(8,128)} %bitcast.1, f32[2,256,256]{2,1,0:T(8,128)} %refs_2_.1, bf16[2,256,256]{2,1,0:T(8,128)(2,1)} %refs_3_.1, bf16[512,512]{1,0:T(8,128)(2,1)} %constant.4.clone.refs_4_, ...), custom_call_target="tpu_custom_call" | custom-call | tf_op jit(solution)/shard_map/whole/pallas_call | solution.py:761
  35.1 1.0 %emit.1 = (f32[2,256,256]{2,1,0:T(8,128)}, f32[2,256,256]{2,1,0:T(8,128)}) custom-call(f32[2,256,256]{2,1,0:T(8,128)S(1)} %get-tuple-element.4.spec, f32[2,256,256]{2,1,0:T(8,128)S(1)} %get-tuple-element.5.probe), custom_call_target="tpu_custom_call" | custom-call | tf_op jit(solution)/shard_map/emit/pallas_call | solution.py:802

commit v10 on v9

--- a/solution.py
+++ b/solution.py
@@ -695,8 +695,9 @@
         fold.send_rims(1)
 
     pl.when(jnp.logical_not(probe_sum.has_outer))(strips_in)
-    probe_sum.three(range(chunks))
+    probe_sum.three(range(chunks - chunks // 4))
     pl.when(probe_sum.has_outer)(strips_in)
+    probe_sum.three(range(chunks - chunks // 4, chunks))
     light.arrive()
     fold.fold(1)
     q4 = fold.q4

time: 36.3 us -> 36.3 us (level)
  no operation moved by 1% of the time
where the time goes in v10:
time: 36.3 us; the launch traced here: 36.2 us
  Pallas kernels  35.5 us (98%)
  between operations  0.64 us (2%)
    pallas_call x1, Pallas kernels, shards(): pl.pallas_call(functools.partial(whole_kernel, nx, ny, step_size), out_sh...  34.5 us
    pallas_call x1, Pallas kernels, shards(): pl.pallas_call(emit_kernel, out_shape=[jax.ShapeDtypeStruct(specimen.shap...  1.03 us

profile of v10, /device:TPU:0, one launch (start us, length us, event | category | flops | bytes accessed | tf_op | source)
XLA Modules:
  0.0 36.2 jit_solution(12033435809105795037)
XLA Ops:
  0.6 34.5 %whole.1 = (f32[2,256,256]{2,1,0:T(8,128)S(1)}, f32[2,256,256]{2,1,0:T(8,128)S(1)}) custom-call(s32[2,2]{1,0:T(2,128)} %refs_0_.1, f32[2,32,8,256]{3,2,1,0:T(8,128)} %bitcast.1, f32[2,256,256]{2,1,0:T(8,128)} %refs_2_.1, bf16[2,256,256]{2,1,0:T(8,128)(2,1)} %refs_3_.1, bf16[512,512]{1,0:T(8,128)(2,1)} %constant.4.clone.refs_4_, ...), custom_call_target="tpu_custom_call" | custom-call | tf_op jit(solution)/shard_map/whole/pallas_call | solution.py:762
  35.1 1.0 %emit.1 = (f32[2,256,256]{2,1,0:T(8,128)}, f32[2,256,256]{2,1,0:T(8,128)}) custom-call(f32[2,256,256]{2,1,0:T(8,128)S(1)} %get-tuple-element.4.spec, f32[2,256,256]{2,1,0:T(8,128)S(1)} %get-tuple-element.5.probe), custom_call_target="tpu_custom_call" | custom-call | tf_op jit(solution)/shard_map/emit/pallas_call | solution.py:803

commit v11 on v10

--- a/solution.py
+++ b/solution.py
@@ -698,6 +698,7 @@
     probe_sum.three(range(chunks - chunks // 4))
     pl.when(probe_sum.has_outer)(strips_in)
     probe_sum.three(range(chunks - chunks // 4, chunks))
+    pl.when(probe_sum.has_outer)(probe_sum.four)
     light.arrive()
     fold.fold(1)
     q4 = fold.q4
@@ -707,7 +708,7 @@
             old = pad[p, (half + r0) // 8 : (half + r0 + h) // 8, :, half : half + tile].reshape(h, tile)
             new_spec[p, r0 : r0 + h] = old + acc[1 + g, b, :, q4 : 3 * q4] / (light_all[b, g, 0] + 1.0)
     share_copy(p).start()
-    probe_sum.four()
+    pl.when(jnp.logical_not(probe_sum.has_outer))(probe_sum.four)
     probe_sum.shared()
     share_copy(1 - p).wait_recv()
     share_copy(p).wait_send()

time: 36.3 us -> 36.3 us (level)
  no operation moved by 1% of the time
where the time goes in v11:
time: 36.3 us; the launch traced here: 36.2 us
  Pallas kernels  35.5 us (98%)
  between operations  0.64 us (2%)
    pallas_call x1, Pallas kernels, shards(): pl.pallas_call(functools.partial(whole_kernel, nx, ny, step_size), out_sh...  34.5 us
    pallas_call x1, Pallas kernels, shards(): pl.pallas_call(emit_kernel, out_shape=[jax.ShapeDtypeStruct(specimen.shap...  1.03 us

profile of v11, /device:TPU:0, one launch (start us, length us, event | category | flops | bytes accessed | tf_op | source)
XLA Modules:
  0.0 36.2 jit_solution(12693862200925661045)
XLA Ops:
  0.6 34.5 %whole.1 = (f32[2,256,256]{2,1,0:T(8,128)S(1)}, f32[2,256,256]{2,1,0:T(8,128)S(1)}) custom-call(s32[2,2]{1,0:T(2,128)} %refs_0_.1, f32[2,32,8,256]{3,2,1,0:T(8,128)} %bitcast.1, f32[2,256,256]{2,1,0:T(8,128)} %refs_2_.1, bf16[2,256,256]{2,1,0:T(8,128)(2,1)} %refs_3_.1, bf16[512,512]{1,0:T(8,128)(2,1)} %constant.4.clone.refs_4_, ...), custom_call_target="tpu_custom_call" | custom-call | tf_op jit(solution)/shard_map/whole/pallas_call | solution.py:763
  35.1 1.0 %emit.1 = (f32[2,256,256]{2,1,0:T(8,128)}, f32[2,256,256]{2,1,0:T(8,128)}) custom-call(f32[2,256,256]{2,1,0:T(8,128)S(1)} %get-tuple-element.4.spec, f32[2,256,256]{2,1,0:T(8,128)S(1)} %get-tuple-element.5.probe), custom_call_target="tpu_custom_call" | custom-call | tf_op jit(solution)/shard_map/emit/pallas_call | solution.py:804
